TPU v7x, 32 devices: a whole 2x2x4 slice. The times are simulated.
32 devices in a mesh: gx: 16 (over z, y, core), gy: 2 (over x).
Axes of the slice: x: 2, y: 2, z: 4, core: 2. Of those that a mesh axis runs over, the one named last changes fastest.
Arguments:
- state_field: bfloat16 [1, 64, 2048, 2048], P(None, None, 'gx', 'gy'), may hold values from -6 to 6
- spectral_x: bfloat16 [2, 32, 2, 64, 64], P(None, 'gx'), may hold values from -2 to 2
- spectral_y: bfloat16 [2, 32, 2, 64, 64], P(None, 'gy'), may hold values from -2 to 2
- expand_weight: bfloat16 [2, 64, 256], replicated, may hold values from -0.75 to 0.75
- reduce_weight: bfloat16 [2, 256, 64], replicated, may hold values from -0.375 to 0.375
Outputs:
- next_state: bfloat16 [1, 64, 2048, 2048], P(None, None, 'gx', 'gy')
All inputs are finite; a program needn't handle non-finite values.
Results may differ from a plain program's by a relative error of at most 0.025.
Values may be sent and summed in bfloat16 or wider, within the bound.
A program may use at most 128 MiB of HBM per device.

v0:
```python
import functools

import jax
import jax.numpy as jnp
from jax import lax
from jax.experimental import pallas as pl
from jax.experimental.pallas import tpu as pltpu
from jax.sharding import PartitionSpec as P

CHUNKS = 2
LANES = 128
GELU_A = 0.7978845608028654
GELU_B = 0.044715


def local_tables(first, count, length, modes):
    positions = first + jnp.arange(count, dtype=jnp.int32)
    orders = jnp.arange(modes, dtype=jnp.int32)
    phase = orders[:, None] * positions[None, :] % length
    angle = 2.0 * jnp.pi * phase.astype(jnp.float32) / length
    factor = 1.0 / jnp.sqrt(jnp.float32(length))
    weight_two = jnp.where(orders == 0, 1.0, 2.0).astype(jnp.float32)[:, None]
    real, imag = jnp.cos(angle) * factor, -jnp.sin(angle) * factor
    forward = jnp.stack([real, imag], axis=1).reshape(2 * modes, count)
    inverse = jnp.stack([weight_two * real, weight_two * imag], axis=1)
    inverse = inverse.reshape(2 * modes, count)
    return forward.astype(jnp.bfloat16), inverse.astype(jnp.bfloat16)


def dot(left, right):
    return jnp.dot(left, right, preferred_element_type=jnp.float32)


def group_spectra(base, news, fx, fyt, s_ref, acc_ref):
    rows2 = fx.shape[0]
    count, rows = len(news), news[0].shape[0]
    wide = dot(fx, jnp.concatenate(news, axis=1))
    for i in range(count):
        s_ref[pl.ds((base + i) * rows2, rows2), :] = wide[:, i * LANES : (i + 1) * LANES]
    tall = dot(jnp.concatenate(news, axis=0), fyt)
    for i in range(count):
        acc_ref[base + i] = acc_ref[base + i] + tall[i * rows : (i + 1) * rows]


def write_spectra(specx_ref, specy_ref, s_ref, acc_ref):
    rows2, channels, _ = specx_ref.shape
    for k in range(rows2):
        specx_ref[k] = s_ref[pl.ds(k, channels, stride=rows2), :].astype(jnp.bfloat16)

    @pl.when(pl.program_id(0) == pl.num_programs(0) - 1)
    def _():
        specy_ref[...] = acc_ref[...].astype(jnp.bfloat16)


def clear_first(acc_ref):
    @pl.when(pl.program_id(0) == 0)
    def _():
        acc_ref[...] = jnp.zeros_like(acc_ref)


def first_kernel(state_ref, fx_ref, fyt_ref, specx_ref, specy_ref, s_ref, acc_ref):
    clear_first(acc_ref)
    fx, fyt = fx_ref[...], fyt_ref[...]

    @pl.loop(0, state_ref.shape[0] // 4)
    def _(g):
        base = g * 4
        group_spectra(base, [state_ref[base + i] for i in range(4)], fx, fyt, s_ref, acc_ref)

    write_spectra(specx_ref, specy_ref, s_ref, acc_ref)


def layer_kernel(last, state_ref, mixed_ref, a_ref, iy_ref, w1_ref, w2_ref, *refs):
    if last:
        out_ref, m_ref, t_ref = refs[-3:]
    else:
        fx_ref, fyt_ref, out_ref, specx_ref, specy_ref, m_ref, t_ref, s_ref, acc_ref = refs
        clear_first(acc_ref)
        fx, fyt = fx_ref[...], fyt_ref[...]
    channels, rows, _ = state_ref.shape
    rows2 = mixed_ref.shape[0]
    for k in range(rows2):
        m_ref[pl.ds(k * channels, channels), :] = mixed_ref[k].astype(jnp.float32)
    iy = iy_ref[...]

    @pl.loop(0, channels // 4)
    def _(g):
        for i in range(4):
            c = g * 4 + i
            part = m_ref[pl.ds(c, rows2, stride=channels), :].astype(jnp.bfloat16)
            t_ref[pl.ds(c * rows, rows), :] = dot(a_ref[c], jnp.concatenate([part, iy], axis=0))

    w1, w2 = w1_ref[...], w2_ref[...]
    ca = jnp.bfloat16(GELU_A)
    cb = jnp.bfloat16(GELU_A * GELU_B)

    @pl.loop(0, rows // 8)
    def _(g):
        for j in range(2):
            base = g * 8 + j * 4
            parts = [t_ref[pl.ds(base + i, channels, stride=rows), :] for i in range(4)]
            h = dot(w1, jnp.concatenate(parts, axis=1).astype(jnp.bfloat16)).astype(jnp.bfloat16)
            th = jnp.tanh(h * (ca + cb * (h * h)))
            u = dot(w2, h + h * th)
            for i in range(4):
                t_ref[pl.ds(base + i, channels, stride=rows), :] = u[:, i * LANES : (i + 1) * LANES]

    @pl.loop(0, channels // 4)
    def _(g):
        base = g * 4
        news = []
        for i in range(4):
            c = base + i
            new = state_ref[c].astype(jnp.float32) + t_ref[pl.ds(c * rows, rows), :]
            new = new.astype(jnp.bfloat16)
            out_ref[c] = new
            news.append(new)
        if not last:
            group_spectra(base, news, fx, fyt, s_ref, acc_ref)

    if not last:
        write_spectra(specx_ref, specy_ref, s_ref, acc_ref)


def whole(array):
    zeros = (0,) * array.ndim
    return pl.BlockSpec(array.shape, lambda j: zeros)


def body(state_field, spectral_x, spectral_y, expand_weight, reduce_weight):
    planes, channels, rows, cols = state_field.shape
    layers, hidden = expand_weight.shape[0], expand_weight.shape[2]
    nx, ny = rows * lax.axis_size("gx"), cols * lax.axis_size("gy")
    modes = spectral_x.shape[1] * lax.axis_size("gx")
    rows2 = 2 * modes
    chunks = CHUNKS if cols % (CHUNKS * LANES) == 0 else cols // LANES
    width = cols // chunks
    steps = width // LANES
    forward_x, inverse_x = local_tables(lax.axis_index("gx") * rows, rows, nx, modes)
    forward_y, inverse_y = local_tables(lax.axis_index("gy") * cols, cols, ny, modes)
    forward_yt = forward_y.T
    inverse_xt = inverse_x.T

    def block_matrix(w):
        top = jnp.concatenate([w[..., 0, :, :], -w[..., 1, :, :]], axis=-1)
        low = jnp.concatenate([w[..., 1, :, :], w[..., 0, :, :]], axis=-1)
        return jnp.concatenate([top, low], axis=-2)

    mat_x = block_matrix(spectral_x)
    mat_y = block_matrix(lax.all_gather(spectral_y, "gy", axis=1, tiled=True))

    bf16 = jnp.bfloat16
    s_scr = pltpu.VMEM((channels * rows2, LANES), jnp.float32)
    m_scr = pltpu.VMEM((rows2 * channels, LANES), jnp.float32)
    t_scr = pltpu.VMEM((channels * rows, LANES), jnp.float32)
    acc_scr = pltpu.VMEM((channels, rows, rows2), jnp.float32)
    specx_shape = jax.ShapeDtypeStruct((rows2, channels, width), bf16)
    specx_spec = pl.BlockSpec((rows2, channels, LANES), lambda j: (0, 0, j))
    specy_shape = jax.ShapeDtypeStruct((channels, rows, rows2), bf16)
    specy_spec = pl.BlockSpec((channels, rows, rows2), lambda j: (0, 0, 0))
    params = pltpu.CompilerParams(
        dimension_semantics=("arbitrary",), vmem_limit_bytes=56 * 1024 * 1024
    )
    cells = rows * width

    def cost(flops, moved):
        return pl.CostEstimate(flops=flops, bytes_accessed=moved, transcendentals=0)

    def at(first):
        return pl.BlockSpec((channels, rows, LANES), lambda j: (0, 0, j + first))

    def fyt_spec(first):
        return pl.BlockSpec((LANES, rows2), lambda j: (j + first, 0))

    spectra_flops = 4 * rows2 * channels * cells

    def first_call(state, n):
        return pl.pallas_call(
            first_kernel,
            name="spectra",
            grid=(steps,),
            in_specs=[at(n * steps), whole(forward_x), fyt_spec(n * steps)],
            out_specs=[specx_spec, specy_spec],
            out_shape=[specx_shape, specy_shape],
            scratch_shapes=[s_scr, acc_scr],
            compiler_params=params,
            cost_estimate=cost(spectra_flops, 4 * channels * cells),
        )(state, forward_x, forward_yt)

    def layer_call(last, state, first, n, mixed, a, w1, w2, result):
        ins = [state, mixed, a, inverse_y, w1, w2]
        specs = [
            at(first),
            specx_spec,
            whole(a),
            pl.BlockSpec((rows2, LANES), lambda j: (0, j + n * steps)),
            whole(w1),
            whole(w2),
        ]
        aliases = {}
        scratch = [m_scr, t_scr]
        if last:
            out_shape = [jax.ShapeDtypeStruct((channels, rows, cols), bf16)]
            out_specs = [at(n * steps)]
            if result is not None:
                aliases = {len(ins): 0}
                ins.append(result)
                specs.append(pl.BlockSpec(memory_space=pl.ANY))
        else:
            ins += [forward_x, forward_yt]
            specs += [whole(forward_x), fyt_spec(n * steps)]
            out_shape = [jax.ShapeDtypeStruct((channels, rows, width), bf16), specx_shape, specy_shape]
            out_specs = [at(0), specx_spec, specy_spec]
            scratch += [s_scr, acc_scr]
        flops = (4 * channels * hidden * 2 + 8 * rows2 * channels) * cells
        return pl.pallas_call(
            functools.partial(layer_kernel, last),
            name="layer_last" if last else "layer",
            grid=(steps,),
            in_specs=specs,
            out_specs=out_specs,
            out_shape=out_shape,
            scratch_shapes=scratch,
            input_output_aliases=aliases,
            compiler_params=params,
            cost_estimate=cost(flops, 8 * channels * cells),
        )(*ins)

    state = state_field.reshape(channels, rows, cols)
    pieces = [(state, n * steps) for n in range(chunks)]
    spectra = [first_call(state, n) for n in range(chunks)]
    for layer in range(layers):
        last = layer == layers - 1
        owned = [lax.psum_scatter(s, "gx", scatter_dimension=0, tiled=True) for s, _ in spectra]
        mixed = []
        for part in owned:
            pairs = part.reshape(part.shape[0] // 2, 2 * channels, width)
            product = jnp.einsum(
                "moi,miy->moy", mat_x[layer], pairs, preferred_element_type=jnp.float32
            )
            product = product.astype(bf16).reshape(part.shape)
            mixed.append(lax.all_gather(product, "gx", axis=0, tiled=True))
        spec_y = sum(s.astype(jnp.float32) for _, s in spectra).astype(bf16)
        spec_y = lax.psum(jnp.transpose(spec_y, (2, 0, 1)), "gy")
        mixed_y = jnp.einsum(
            "moi,mix->mox",
            mat_y[layer],
            spec_y.reshape(modes, 2 * channels, rows),
            preferred_element_type=jnp.float32,
        ).astype(bf16)
        mixed_y = jnp.transpose(mixed_y.reshape(rows2, channels, rows), (1, 2, 0))
        a = jnp.concatenate(
            [jnp.broadcast_to(inverse_xt[None], (channels, rows, rows2)), mixed_y], axis=2
        )
        w1 = expand_weight[layer].T
        w2 = (reduce_weight[layer].astype(jnp.float32) * 0.5).astype(bf16).T
        result, next_pieces, next_spectra = None, [], []
        for n in range(chunks):
            source, first = pieces[n]
            outs = layer_call(last, source, first, n, mixed[n], a, w1, w2, result)
            if last:
                result = outs[0]
            else:
                next_pieces.append((outs[0], 0))
                next_spectra.append((outs[1], outs[2]))
        pieces, spectra = next_pieces, next_spectra
    return result.reshape(state_field.shape)


def solution(mesh):
    in_specs = (
        P(None, None, "gx", "gy"),
        P(None, "gx", None, None, None),
        P(None, "gy", None, None, None),
        P(),
        P(),
    )
    out_specs = P(None, None, "gx", "gy")
    return jax.shard_map(body, mesh=mesh, in_specs=in_specs, out_specs=out_specs, check_vma=False)
```

profile of v0, /device:TPU:0, one launch (start us, length us, event | category | flops | bytes accessed | tf_op | source)
XLA Modules:
  0.0 647.1 jit_solution(12769252736048336722)
XLA Ops:
  7.4 0.1 multiply_convert_fusion.7
  7.5 0.6 copy.38
  8.1 0.6 multiply_convert_fusion.1
  8.7 0.1 copy.39
  8.9 0.1 convert_element_type.117
  8.9 0.8 copy.40
  9.8 21.9 %spectra.3 = (bf16[64,64,512]{2,1,0:T(8,128)(2,1)}, bf16[64,128,64]{2,1,0:T(8,128)(2,1)}) custom-call(bf16[64,128,1024]{2,1,0:T(8,128)(2,1)} %bitcast.75, bf16[64,128]{1,0:T(8,128)(2,1)} %bitcast.99, bf16[1024,64]{1,0:T(8,128)(2,1)} %bitcast.85), custom_call_target="tpu_custom_call" | custom-call | flops 1073741824 | bytes 16777216 | tf_op jit(solution)/shard_map/spectra/pallas_call | solution.py:178
  31.7 0.0 reduce-scatter.9.cloned.1.call-update
  31.7 0.0 reduce-scatter.5.cloned.1.call-start
  31.7 21.9 %spectra.2 = (bf16[64,64,512]{2,1,0:T(8,128)(2,1)}, bf16[64,128,64]{2,1,0:T(8,128)(2,1)}) custom-call(bf16[64,128,1024]{2,1,0:T(8,128)(2,1)} %bitcast.76, bf16[64,128]{1,0:T(8,128)(2,1)} %bitcast.100, bf16[1024,64]{1,0:T(8,128)(2,1)} %bitcast.86), custom_call_target="tpu_custom_call" | custom-call | flops 1073741824 | bytes 16777216 | tf_op jit(solution)/shard_map/spectra/pallas_call | solution.py:178
  53.7 0.0 reduce-scatter.5.cloned.1.call-update
  53.7 0.0 all-gather.8.cloned.1.call-start
  53.8 1.2 copy-done.3
  55.0 1.1 copy.43
  56.0 0.0 all-gather.8.cloned.1.call-update
  56.0 0.0 all-reduce.3.cloned.1.call-start
  56.1 3.0 fusion
  59.1 2.5 copy.44
  61.6 0.0 all-reduce.3.cloned.1.call-update
  61.6 0.0 all-gather.12.cloned.1.call-start
  61.7 0.1 maximum_maximum_fusion.1
  61.8 45.6 %reduce-scatter.9.cloned.1.call-done = bf16[4,64,512]{2,1,0:T(8,128)(2,1)} async-done(((bf16[64,64,512]{2,1,0:T(8,128)(2,1)}), bf16[4,64,512]{2,1,0:T(8,128)(2,1)}) %reduce-scatter.9.cloned.1.call-update) | async-done | bytes 262160 | tf_op jit(solution)/shard_map/reduce_scatter | solution.py:234
  107.4 1.9 convolution_convert_fusion.3
  109.3 0.0 all-gather.12.cloned.1.call-update
  109.3 0.0 all-gather.6.cloned.1.call-start
  109.3 86.0 %reduce-scatter.5.cloned.1.call-done = bf16[4,64,512]{2,1,0:T(8,128)(2,1)} async-done(((bf16[64,64,512]{2,1,0:T(8,128)(2,1)}), bf16[4,64,512]{2,1,0:T(8,128)(2,1)}) %reduce-scatter.5.cloned.1.call-update) | async-done | bytes 262160 | tf_op jit(solution)/shard_map/reduce_scatter | solution.py:234
  195.3 1.9 convolution_convert_fusion.5
  197.2 0.0 all-gather.6.cloned.1.call-update
  197.2 0.2 reduce-scatter.11.cloned.1.call-start
  197.5 0.1 copy.42
  197.6 0.7 copy.53
  198.3 0.1 copy.46
  198.5 0.7 convert_element_type.124.iy_ref
  199.2 0.6 fusion.10
  199.8 1.5 fusion.20
  201.3 0.4 copy-done.2
  201.8 0.2 slice_bitcast_fusion.4
  202.0 1.2 maximum_maximum_fusion
  203.2 0.0 all-reduce.3.cloned.1.call-done
  203.2 2.4 convolution_convert_fusion.1
  205.6 2.3 copy.45
  207.9 0.5 broadcast_in_dim.14
  208.4 1.1 copy-done.1
  209.5 2.5 pad_maximum_fusion.1.a_ref
  211.9 89.4 %layer.3 = (bf16[64,128,512]{2,1,0:T(8,128)(2,1)}, bf16[64,64,512]{2,1,0:T(8,128)(2,1)}, bf16[64,128,64]{2,1,0:T(8,128)(2,1)}) custom-call(bf16[64,128,1024]{2,1,0:T(8,128)(2,1)} %bitcast.77, bf16[64,64,512]{2,1,0:T(8,128)(2,1)} %all-gather.12.cloned.1.call-done.mixed_ref, bf16[64,128,128]{2,1,0:T(8,128)(2,1)} %pad_maximum_fusion.1.a_ref, ...), custom_call_target="tpu_custom_call" | custom-call | flops 10737418240 | bytes 33554432 | tf_op jit(solution)/shard_map/layer/pallas_call | solution.py:216
  301.4 0.0 reduce-scatter.7.cloned.1.call-start
  301.4 0.0 all-gather.6.cloned.1.call-done.mixed_ref
  301.5 89.2 %layer.2 = (bf16[64,128,512]{2,1,0:T(8,128)(2,1)}, bf16[64,64,512]{2,1,0:T(8,128)(2,1)}, bf16[64,128,64]{2,1,0:T(8,128)(2,1)}) custom-call(bf16[64,128,1024]{2,1,0:T(8,128)(2,1)} %bitcast.78, bf16[64,64,512]{2,1,0:T(8,128)(2,1)} %all-gather.6.cloned.1.call-done.mixed_ref, bf16[64,128,128]{2,1,0:T(8,128)(2,1)} %pad_maximum_fusion.1.a_ref, ...), custom_call_target="tpu_custom_call" | custom-call | flops 10737418240 | bytes 33554432 | tf_op jit(solution)/shard_map/layer/pallas_call | solution.py:216
  390.7 0.0 all-reduce.5.cloned.1.call-start
  390.8 4.6 fusion.1
  395.4 3.5 copy.48
  399.0 0.0 all-gather.14.cloned.1.call-start
  399.0 0.0 reduce-scatter.11.cloned.1.call-done
  399.1 1.9 convolution_convert_fusion.2
  401.0 0.3 all-gather.10.cloned.1.call-start
  401.2 65.8 %reduce-scatter.7.cloned.1.call-done = bf16[4,64,512]{2,1,0:T(8,128)(2,1)} async-done(((bf16[64,64,512]{2,1,0:T(8,128)(2,1)}), bf16[4,64,512]{2,1,0:T(8,128)(2,1)}) %reduce-scatter.7.cloned.1.call-update) | async-done | bytes 262160 | tf_op jit(solution)/shard_map/reduce_scatter | solution.py:234
  467.1 1.9 convolution_convert_fusion.4
  469.0 0.7 copy.54
  469.7 2.0 convolution_convert_fusion
  471.7 2.3 copy.49
  473.9 4.1 pad_maximum_fusion.a_ref
  478.1 19.2 %all-gather.14.cloned.1.call-done.mixed_ref = bf16[64,64,512]{2,1,0:T(8,128)(2,1)} async-done(((bf16[4,64,512]{2,1,0:T(8,128)(2,1)}), bf16[64,64,512]{2,1,0:T(8,128)(2,1)}) %all-gather.14.cloned.1.call-update) | async-done | bytes 4194320 | tf_op jit(solution)/shard_map/all_gather | solution.py:242
  497.3 71.3 %layer_last.2.refs_0_ = bf16[64,128,1024]{2,1,0:T(8,128)(2,1)} custom-call(bf16[64,128,512]{2,1,0:T(8,128)(2,1)} %get-tuple-element.23.state_ref, bf16[64,64,512]{2,1,0:T(8,128)(2,1)} %all-gather.14.cloned.1.call-done.mixed_ref, bf16[64,128,128]{2,1,0:T(8,128)(2,1)} %pad_maximum_fusion.a_ref, bf16[64,1024]{1,0:T(8,128)(2,1)} %convert_element_type.124.iy_ref, ...), custom_call_target="tpu_custom_call" | custom-call | flops 10737418240 | bytes 33554432 | tf_op jit(solution)/shard_map/layer_last/pallas_call | solution.py:216
  568.6 71.4 %layer_last.3 = bf16[64,128,1024]{2,1,0:T(8,128)(2,1)} custom-call(bf16[64,128,512]{2,1,0:T(8,128)(2,1)} %get-tuple-element.18.state_ref, bf16[64,64,512]{2,1,0:T(8,128)(2,1)} %all-gather.10.cloned.1.call-done.mixed_ref, bf16[64,128,128]{2,1,0:T(8,128)(2,1)} %pad_maximum_fusion.a_ref, ...), custom_call_target="tpu_custom_call", output_to_operand_aliasing={{}: (6, {})} | custom-call | flops 10737418240 | bytes 33554432 | tf_op jit(solution)/shard_map/layer_last/pallas_call | solution.py:216
  (30 shorter events, 0.2 us)
Async XLA Ops:
  7.4 100.0 %reduce-scatter.9.cloned.1.call-start = ((), (), s32[]{:S(2)}) async-start(), calls=%async_computation.10 | async-start | bytes 4456448 | tf_op jit(solution)/shard_map/reduce_scatter | solution.py:234
  31.7 163.6 %reduce-scatter.5.cloned.1.call-start = ((), (), s32[]{:S(2)}) async-start(), calls=%async_computation.4 | async-start | bytes 4456448 | tf_op jit(solution)/shard_map/reduce_scatter | solution.py:234
  53.7 1.3 copy-start.3
  53.7 146.1 %all-gather.8.cloned.1.call-start = ((), (), s32[]{:S(2)}) async-start(), calls=%async_computation.6 | async-start | bytes 3145728 | tf_op jit(solution)/shard_map/all_gather | solution.py:150
  56.0 147.2 %all-reduce.3.cloned.1.call-start = ((), (), s32[]{:S(2)}) async-start(), calls=%async_computation.7 | async-start | bytes 2097152 | tf_op jit(solution)/shard_map/psum | solution.py:244
  59.1 2.6 copy-start.4
  61.6 136.0 %copy-start.5 = (bf16[2,64,256]{2,1,0:T(8,128)(2,1)S(1)}, bf16[2,64,256]{2,1,0:T(8,128)(2,1)}, u32[]{:S(2)}) copy-start(bf16[2,64,256]{2,1,0:T(8,128)(2,1)} %param.8) | copy-start | bytes 196612
  61.6 137.6 %copy-start.6 = (bf16[2,256,64]{1,2,0:T(8,128)(2,1)S(1)}, bf16[2,256,64]{1,2,0:T(8,128)(2,1)}, u32[]{:S(2)}) copy-start(bf16[2,256,64]{1,2,0:T(8,128)(2,1)} %param.9) | copy-start | bytes 196612
  61.6 150.3 %all-gather.12.cloned.1.call-start = ((), (), s32[]{:S(2)}) async-start(), calls=%async_computation.11 | async-start | bytes 4456448 | tf_op jit(solution)/shard_map/all_gather | solution.py:242
  109.3 192.2 %all-gather.6.cloned.1.call-start = ((), (), s32[]{:S(2)}) async-start(), calls=%async_computation.5 | async-start | bytes 4456448 | tf_op jit(solution)/shard_map/all_gather | solution.py:242
  197.2 201.8 %reduce-scatter.11.cloned.1.call-start = ((), (), s32[]{:S(2)}) async-start(), calls=%async_computation.13 | async-start | bytes 4456448 | tf_op jit(solution)/shard_map/reduce_scatter | solution.py:234
  199.8 2.0 copy-start.2
  203.2 2.4 copy-start
  207.9 1.6 copy-start.1
  301.4 165.7 %reduce-scatter.7.cloned.1.call-start = ((), (), s32[]{:S(2)}) async-start(), calls=%async_computation.8 | async-start | bytes 4456448 | tf_op jit(solution)/shard_map/reduce_scatter | solution.py:234
  390.7 79.0 %all-reduce.5.cloned.1.call-start = ((), (), s32[]{:S(2)}) async-start(), calls=%async_computation.12 | async-start | bytes 2097152 | tf_op jit(solution)/shard_map/psum | solution.py:244
  399.0 98.3 %all-gather.14.cloned.1.call-start = ((), (), s32[]{:S(2)}) async-start(), calls=%async_computation.14 | async-start | bytes 4456448 | tf_op jit(solution)/shard_map/all_gather | solution.py:242
  401.0 167.6 %all-gather.10.cloned.1.call-start = ((), (), s32[]{:S(2)}) async-start(), calls=%async_computation.9 | async-start | bytes 4456448 | tf_op jit(solution)/shard_map/all_gather | solution.py:242
Sparse Core Ops, SparseCore 0:
  31.8 75.5 reduce-scatter.8
  111.2 84.0 reduce-scatter.4
  301.5 72.9 reduce-scatter.10
  390.8 76.1 reduce-scatter.6
Sparse Core Ops, SparseCore 1:
  56.1 35.6 all-gather.7
  94.0 39.9 all-reduce.2
  136.0 65.6 all-gather.11
  203.8 49.9 all-gather.5
  399.1 40.1 all-reduce.4
  441.4 55.8 all-gather.13
  499.3 49.1 all-gather.9
where the time goes:
time: 648 us; the launch traced here: 647 us
  Pallas kernels  365 us (56%)
  waiting for transfers between devices  217 us (33%)
  local copies, waits for them, and re-layouts  19.1 us (3%)
  other arithmetic  18.4 us (3%)
  between operations  14.9 us (2%)
  matrix products  11.9 us (2%)
    pallas_call x4, Pallas kernels, layer_call(): pl.pallas_call(functools.partial(layer_kernel, last), name='layer_last' i...  321 us
    reduce_scatter x4, waiting for transfers between devices, body(): lax.psum_scatter(s, 'gx', scatter_dimension=0, tiled=True)  197 us
    pallas_call x2, Pallas kernels, first_call(): pl.pallas_call(first_kernel, name='spectra', grid=(steps,), in_specs=[at(...  43.9 us
    all_gather x4, waiting for transfers between devices, body(): mixed.append(lax.all_gather(product, 'gx', axis=0, tiled=True))  19.3 us
  transfers between devices with their start and end apart: 11, of which 4 were waited for; matrix products, arithmetic and copies ran while one was open for 7% of the time, Pallas kernels for 42%

commit v1 on v0

--- a/solution.py
+++ b/solution.py
@@ -9,8 +9,10 @@
 
 CHUNKS = 2
 LANES = 128
+PAD = 4
 GELU_A = 0.7978845608028654
 GELU_B = 0.044715
+GELU_S = (GELU_A * GELU_B) ** (1.0 / 3.0)
 
 
 def local_tables(first, count, length, modes):
@@ -36,7 +38,7 @@
     count, rows = len(news), news[0].shape[0]
     wide = dot(fx, jnp.concatenate(news, axis=1))
     for i in range(count):
-        s_ref[pl.ds((base + i) * rows2, rows2), :] = wide[:, i * LANES : (i + 1) * LANES]
+        s_ref[pl.ds((base + i) * (rows2 + PAD), rows2), :] = wide[:, i * LANES : (i + 1) * LANES]
     tall = dot(jnp.concatenate(news, axis=0), fyt)
     for i in range(count):
         acc_ref[base + i] = acc_ref[base + i] + tall[i * rows : (i + 1) * rows]
@@ -45,7 +47,7 @@
 def write_spectra(specx_ref, specy_ref, s_ref, acc_ref):
     rows2, channels, _ = specx_ref.shape
     for k in range(rows2):
-        specx_ref[k] = s_ref[pl.ds(k, channels, stride=rows2), :].astype(jnp.bfloat16)
+        specx_ref[k] = s_ref[pl.ds(k, channels, stride=rows2 + PAD), :].astype(jnp.bfloat16)
 
     @pl.when(pl.program_id(0) == pl.num_programs(0) - 1)
     def _():
@@ -79,31 +81,29 @@
         fx, fyt = fx_ref[...], fyt_ref[...]
     channels, rows, _ = state_ref.shape
     rows2 = mixed_ref.shape[0]
+    t_step, m_step = rows + PAD, channels + PAD
     for k in range(rows2):
-        m_ref[pl.ds(k * channels, channels), :] = mixed_ref[k].astype(jnp.float32)
+        m_ref[pl.ds(k * m_step, channels), :] = mixed_ref[k].astype(jnp.float32)
     iy = iy_ref[...]
 
     @pl.loop(0, channels // 4)
     def _(g):
         for i in range(4):
             c = g * 4 + i
-            part = m_ref[pl.ds(c, rows2, stride=channels), :].astype(jnp.bfloat16)
-            t_ref[pl.ds(c * rows, rows), :] = dot(a_ref[c], jnp.concatenate([part, iy], axis=0))
+            part = m_ref[pl.ds(c, rows2, stride=m_step), :].astype(jnp.bfloat16)
+            t_ref[pl.ds(c * t_step, rows), :] = dot(a_ref[c], jnp.concatenate([part, iy], axis=0))
 
     w1, w2 = w1_ref[...], w2_ref[...]
-    ca = jnp.bfloat16(GELU_A)
-    cb = jnp.bfloat16(GELU_A * GELU_B)
+    cg = jnp.bfloat16(GELU_A / GELU_S)
 
     @pl.loop(0, rows // 8)
     def _(g):
-        for j in range(2):
-            base = g * 8 + j * 4
-            parts = [t_ref[pl.ds(base + i, channels, stride=rows), :] for i in range(4)]
-            h = dot(w1, jnp.concatenate(parts, axis=1).astype(jnp.bfloat16)).astype(jnp.bfloat16)
-            th = jnp.tanh(h * (ca + cb * (h * h)))
-            u = dot(w2, h + h * th)
-            for i in range(4):
-                t_ref[pl.ds(base + i, channels, stride=rows), :] = u[:, i * LANES : (i + 1) * LANES]
+        base = g * 8
+        parts = [t_ref[pl.ds(base + i, channels, stride=t_step), :] for i in range(8)]
+        h = dot(w1, jnp.concatenate(parts, axis=1).astype(jnp.bfloat16)).astype(jnp.bfloat16)
+        u = dot(w2, h + h * jnp.tanh(h * (h * h + cg)))
+        for i in range(8):
+            t_ref[pl.ds(base + i, channels, stride=t_step), :] = u[:, i * LANES : (i + 1) * LANES]
 
     @pl.loop(0, channels // 4)
     def _(g):
@@ -111,7 +111,7 @@
         news = []
         for i in range(4):
             c = base + i
-            new = state_ref[c].astype(jnp.float32) + t_ref[pl.ds(c * rows, rows), :]
+            new = state_ref[c].astype(jnp.float32) + t_ref[pl.ds(c * t_step, rows), :]
             new = new.astype(jnp.bfloat16)
             out_ref[c] = new
             news.append(new)
@@ -150,9 +150,9 @@
     mat_y = block_matrix(lax.all_gather(spectral_y, "gy", axis=1, tiled=True))
 
     bf16 = jnp.bfloat16
-    s_scr = pltpu.VMEM((channels * rows2, LANES), jnp.float32)
-    m_scr = pltpu.VMEM((rows2 * channels, LANES), jnp.float32)
-    t_scr = pltpu.VMEM((channels * rows, LANES), jnp.float32)
+    s_scr = pltpu.VMEM((channels * (rows2 + PAD), LANES), jnp.float32)
+    m_scr = pltpu.VMEM((rows2 * (channels + PAD), LANES), jnp.float32)
+    t_scr = pltpu.VMEM((channels * (rows + PAD), LANES), jnp.float32)
     acc_scr = pltpu.VMEM((channels, rows, rows2), jnp.float32)
     specx_shape = jax.ShapeDtypeStruct((rows2, channels, width), bf16)
     specx_spec = pl.BlockSpec((rows2, channels, LANES), lambda j: (0, 0, j))
@@ -252,8 +252,8 @@
         a = jnp.concatenate(
             [jnp.broadcast_to(inverse_xt[None], (channels, rows, rows2)), mixed_y], axis=2
         )
-        w1 = expand_weight[layer].T
-        w2 = (reduce_weight[layer].astype(jnp.float32) * 0.5).astype(bf16).T
+        w1 = (expand_weight[layer].astype(jnp.float32) * GELU_S).astype(bf16).T
+        w2 = (reduce_weight[layer].astype(jnp.float32) * (0.5 / GELU_S)).astype(bf16).T
         result, next_pieces, next_spectra = None, [], []
         for n in range(chunks):
             source, first = pieces[n]

time: 648 us -> 543 us (0.84)
  Pallas kernels: 365 us -> 248 us
  waiting for transfers between devices: 217 us -> 229 us
    pallas_call x4, Pallas kernels: 321 us -> 213 us  [layer_call(): pl.pallas_call(functools.partial(layer_kernel, last), name='layer_last' i...]
    reduce_scatter x4, waiting for transfers between devices: 197 us -> 227 us  [body(): lax.psum_scatter(s, 'gx', scatter_dimension=0, tiled=True)]
    all_gather x4, waiting for transfers between devices: 19.3 us -> 1.43 us  [body(): mixed.append(lax.all_gather(product, 'gx', axis=0, tiled=True))]
    pallas_call x2, Pallas kernels: 43.9 us -> 35.6 us  [first_call(): pl.pallas_call(first_kernel, name='spectra', grid=(steps,), in_specs=[at(...]
  transfers between devices with their start and end apart: 11 -> 11, of which waited for: 4 -> 5; matrix products, arithmetic and copies ran while one was open for 7% -> 8% of each run, Pallas kernels for 42% -> 34%
where the time goes in v1:
time: 543 us; the launch traced here: 542 us
  Pallas kernels  248 us (46%)
  waiting for transfers between devices  229 us (42%)
  other arithmetic  19.9 us (4%)
  local copies, waits for them, and re-layouts  17.8 us (3%)
  between operations  14.9 us (3%)
  matrix products  11.9 us (2%)
    reduce_scatter x4, waiting for transfers between devices, body(): lax.psum_scatter(s, 'gx', scatter_dimension=0, tiled=True)  227 us
    pallas_call x4, Pallas kernels, layer_call(): pl.pallas_call(functools.partial(layer_kernel, last), name='layer_last' i...  213 us
    pallas_call x2, Pallas kernels, first_call(): pl.pallas_call(first_kernel, name='spectra', grid=(steps,), in_specs=[at(...  35.6 us
  transfers between devices with their start and end apart: 11, of which 5 were waited for; matrix products, arithmetic and copies ran while one was open for 8% of the time, Pallas kernels for 34%

profile of v1, /device:TPU:0, one launch (start us, length us, event | category | flops | bytes accessed | tf_op | source)
XLA Modules:
  0.0 542.3 jit_solution(9058008054924084320)
XLA Ops:
  7.4 0.1 multiply_convert_fusion.9
  7.5 0.6 copy.38
  8.1 0.6 multiply_convert_fusion.3
  8.7 0.1 copy.39
  8.9 0.1 convert_element_type.137
  8.9 0.8 copy.40
  9.8 17.8 %spectra.3 = (bf16[64,64,512]{2,1,0:T(8,128)(2,1)}, bf16[64,128,64]{2,1,0:T(8,128)(2,1)}) custom-call(bf16[64,128,1024]{2,1,0:T(8,128)(2,1)} %bitcast.77, bf16[64,128]{1,0:T(8,128)(2,1)} %bitcast.99, bf16[1024,64]{1,0:T(8,128)(2,1)} %bitcast.87), custom_call_target="tpu_custom_call" | custom-call | flops 1073741824 | bytes 16777216 | tf_op jit(solution)/shard_map/spectra/pallas_call | solution.py:178
  27.5 0.0 reduce-scatter.9.cloned.1.call-update
  27.5 0.0 reduce-scatter.5.cloned.1.call-start
  27.6 17.8 %spectra.2 = (bf16[64,64,512]{2,1,0:T(8,128)(2,1)}, bf16[64,128,64]{2,1,0:T(8,128)(2,1)}) custom-call(bf16[64,128,1024]{2,1,0:T(8,128)(2,1)} %bitcast.78, bf16[64,128]{1,0:T(8,128)(2,1)} %bitcast.100, bf16[1024,64]{1,0:T(8,128)(2,1)} %bitcast.88), custom_call_target="tpu_custom_call" | custom-call | flops 1073741824 | bytes 16777216 | tf_op jit(solution)/shard_map/spectra/pallas_call | solution.py:178
  45.4 0.0 reduce-scatter.5.cloned.1.call-update
  45.4 0.0 all-gather.8.cloned.1.call-start
  45.5 1.2 copy-done.3
  46.7 1.1 copy.43
  47.8 0.0 all-reduce.3.cloned.1.call-start
  47.8 3.2 fusion
  51.0 2.5 copy.44
  53.5 0.0 all-gather.12.cloned.1.call-start
  53.6 0.1 maximum_maximum_fusion.1
  53.7 49.5 %reduce-scatter.9.cloned.1.call-done = bf16[4,64,512]{2,1,0:T(8,128)(2,1)} async-done(((bf16[64,64,512]{2,1,0:T(8,128)(2,1)}), bf16[4,64,512]{2,1,0:T(8,128)(2,1)}) %reduce-scatter.9.cloned.1.call-update) | async-done | bytes 262160 | tf_op jit(solution)/shard_map/reduce_scatter | solution.py:234
  103.3 1.9 convolution_convert_fusion.3
  105.2 0.0 all-gather.6.cloned.1.call-start
  105.2 86.0 %reduce-scatter.5.cloned.1.call-done = bf16[4,64,512]{2,1,0:T(8,128)(2,1)} async-done(((bf16[64,64,512]{2,1,0:T(8,128)(2,1)}), bf16[4,64,512]{2,1,0:T(8,128)(2,1)}) %reduce-scatter.5.cloned.1.call-update) | async-done | bytes 262160 | tf_op jit(solution)/shard_map/reduce_scatter | solution.py:234
  191.2 1.9 convolution_convert_fusion.5
  193.1 0.0 reduce-scatter.11.cloned.1.call-start
  193.2 0.1 copy.42
  193.3 0.1 copy.53
  193.4 0.1 copy.46
  193.6 0.7 convert_element_type.144.iy_ref
  194.3 0.6 fusion.12
  194.9 0.6 fusion.8.w1_ref
  195.6 1.5 fusion.22
  197.1 0.4 copy-done.2
  197.5 0.2 slice_bitcast_fusion.4
  197.7 1.2 maximum_maximum_fusion
  198.9 0.0 all-reduce.3.cloned.1.call-done
  198.9 2.4 convolution_convert_fusion.1
  201.3 2.3 copy.45
  203.6 0.5 broadcast_in_dim.14
  204.1 1.1 copy-done.1
  205.2 2.5 pad_maximum_fusion.1.a_ref
  207.7 60.3 %layer.3 = (bf16[64,128,512]{2,1,0:T(8,128)(2,1)}, bf16[64,64,512]{2,1,0:T(8,128)(2,1)}, bf16[64,128,64]{2,1,0:T(8,128)(2,1)}) custom-call(bf16[64,128,1024]{2,1,0:T(8,128)(2,1)} %bitcast.79, bf16[64,64,512]{2,1,0:T(8,128)(2,1)} %all-gather.12.cloned.1.call-done.mixed_ref, bf16[64,128,128]{2,1,0:T(8,128)(2,1)} %pad_maximum_fusion.1.a_ref, ...), custom_call_target="tpu_custom_call" | custom-call | flops 10737418240 | bytes 33554432 | tf_op jit(solution)/shard_map/layer/pallas_call | solution.py:216
  268.0 0.2 reduce-scatter.7.cloned.1.call-start
  268.3 0.0 all-gather.6.cloned.1.call-done.mixed_ref
  268.3 60.1 %layer.2 = (bf16[64,128,512]{2,1,0:T(8,128)(2,1)}, bf16[64,64,512]{2,1,0:T(8,128)(2,1)}, bf16[64,128,64]{2,1,0:T(8,128)(2,1)}) custom-call(bf16[64,128,1024]{2,1,0:T(8,128)(2,1)} %bitcast.80, bf16[64,64,512]{2,1,0:T(8,128)(2,1)} %all-gather.6.cloned.1.call-done.mixed_ref, bf16[64,128,128]{2,1,0:T(8,128)(2,1)} %pad_maximum_fusion.1.a_ref, ...), custom_call_target="tpu_custom_call" | custom-call | flops 10737418240 | bytes 33554432 | tf_op jit(solution)/shard_map/layer/pallas_call | solution.py:216
  328.5 0.0 all-reduce.5.cloned.1.call-start
  328.5 4.6 fusion.1
  333.2 3.5 copy.48
  336.6 0.0 all-reduce.5.cloned.1.call-update
  336.6 0.0 all-gather.14.cloned.1.call-start
  336.7 4.8 reduce-scatter.11.cloned.1.call-done
  341.5 1.9 convolution_convert_fusion.2
  343.4 0.0 all-gather.10.cloned.1.call-start
  343.5 87.0 %reduce-scatter.7.cloned.1.call-done = bf16[4,64,512]{2,1,0:T(8,128)(2,1)} async-done(((bf16[64,64,512]{2,1,0:T(8,128)(2,1)}), bf16[4,64,512]{2,1,0:T(8,128)(2,1)}) %reduce-scatter.7.cloned.1.call-update) | async-done | bytes 262160 | tf_op jit(solution)/shard_map/reduce_scatter | solution.py:234
  430.5 1.9 convolution_convert_fusion.4
  432.3 0.0 all-gather.10.cloned.1.call-update
  432.4 0.1 copy.54
  432.5 0.6 fusion.9.w1_ref
  433.1 2.0 convolution_convert_fusion
  435.1 2.3 copy.49
  437.4 4.1 pad_maximum_fusion.a_ref
  441.5 46.1 %layer_last.2.refs_0_ = bf16[64,128,1024]{2,1,0:T(8,128)(2,1)} custom-call(bf16[64,128,512]{2,1,0:T(8,128)(2,1)} %get-tuple-element.23.state_ref, bf16[64,64,512]{2,1,0:T(8,128)(2,1)} %all-gather.14.cloned.1.call-done.mixed_ref, bf16[64,128,128]{2,1,0:T(8,128)(2,1)} %pad_maximum_fusion.a_ref, bf16[64,1024]{1,0:T(8,128)(2,1)} %convert_element_type.144.iy_ref, ...), custom_call_target="tpu_custom_call" | custom-call | flops 10737418240 | bytes 33554432 | tf_op jit(solution)/shard_map/layer_last/pallas_call | solution.py:216
  487.6 1.4 all-gather.10.cloned.1.call-done.mixed_ref
  489.0 46.2 %layer_last.3 = bf16[64,128,1024]{2,1,0:T(8,128)(2,1)} custom-call(bf16[64,128,512]{2,1,0:T(8,128)(2,1)} %get-tuple-element.18.state_ref, bf16[64,64,512]{2,1,0:T(8,128)(2,1)} %all-gather.10.cloned.1.call-done.mixed_ref, bf16[64,128,128]{2,1,0:T(8,128)(2,1)} %pad_maximum_fusion.a_ref, ...), custom_call_target="tpu_custom_call", output_to_operand_aliasing={{}: (6, {})} | custom-call | flops 10737418240 | bytes 33554432 | tf_op jit(solution)/shard_map/layer_last/pallas_call | solution.py:216
  (32 shorter events, 0.2 us)
Async XLA Ops:
  7.4 95.9 %reduce-scatter.9.cloned.1.call-start = ((), (), s32[]{:S(2)}) async-start(), calls=%async_computation.10 | async-start | bytes 4456448 | tf_op jit(solution)/shard_map/reduce_scatter | solution.py:234
  27.5 163.7 %reduce-scatter.5.cloned.1.call-start = ((), (), s32[]{:S(2)}) async-start(), calls=%async_computation.4 | async-start | bytes 4456448 | tf_op jit(solution)/shard_map/reduce_scatter | solution.py:234
  45.4 1.3 copy-start.3
  45.4 150.2 %all-gather.8.cloned.1.call-start = ((), (), s32[]{:S(2)}) async-start(), calls=%async_computation.6 | async-start | bytes 3145728 | tf_op jit(solution)/shard_map/all_gather | solution.py:150
  47.8 151.2 %all-reduce.3.cloned.1.call-start = ((), (), s32[]{:S(2)}) async-start(), calls=%async_computation.7 | async-start | bytes 2097152 | tf_op jit(solution)/shard_map/psum | solution.py:244
  51.0 2.6 copy-start.4
  53.5 139.8 %copy-start.5 = (bf16[2,64,256]{2,1,0:T(8,128)(2,1)S(1)}, bf16[2,64,256]{2,1,0:T(8,128)(2,1)}, u32[]{:S(2)}) copy-start(bf16[2,64,256]{2,1,0:T(8,128)(2,1)} %param.8) | copy-start | bytes 196612
  53.5 140.8 %copy-start.6 = (bf16[2,256,64]{1,2,0:T(8,128)(2,1)S(1)}, bf16[2,256,64]{1,2,0:T(8,128)(2,1)}, u32[]{:S(2)}) copy-start(bf16[2,256,64]{1,2,0:T(8,128)(2,1)} %param.9) | copy-start | bytes 196612
  53.5 154.1 %all-gather.12.cloned.1.call-start = ((), (), s32[]{:S(2)}) async-start(), calls=%async_computation.11 | async-start | bytes 4456448 | tf_op jit(solution)/shard_map/all_gather | solution.py:242
  105.2 163.1 %all-gather.6.cloned.1.call-start = ((), (), s32[]{:S(2)}) async-start(), calls=%async_computation.5 | async-start | bytes 4456448 | tf_op jit(solution)/shard_map/all_gather | solution.py:242
  193.1 148.4 %reduce-scatter.11.cloned.1.call-start = ((), (), s32[]{:S(2)}) async-start(), calls=%async_computation.13 | async-start | bytes 4456448 | tf_op jit(solution)/shard_map/reduce_scatter | solution.py:234
  195.6 2.0 copy-start.2
  198.9 2.4 copy-start
  203.6 1.6 copy-start.1
  268.0 162.4 %reduce-scatter.7.cloned.1.call-start = ((), (), s32[]{:S(2)}) async-start(), calls=%async_computation.8 | async-start | bytes 4456448 | tf_op jit(solution)/shard_map/reduce_scatter | solution.py:234
  328.5 104.7 %all-reduce.5.cloned.1.call-start = ((), (), s32[]{:S(2)}) async-start(), calls=%async_computation.12 | async-start | bytes 2097152 | tf_op jit(solution)/shard_map/psum | solution.py:244
  336.6 104.9 %all-gather.14.cloned.1.call-start = ((), (), s32[]{:S(2)}) async-start(), calls=%async_computation.14 | async-start | bytes 4456448 | tf_op jit(solution)/shard_map/all_gather | solution.py:242
  343.4 145.6 %all-gather.10.cloned.1.call-start = ((), (), s32[]{:S(2)}) async-start(), calls=%async_computation.9 | async-start | bytes 4456448 | tf_op jit(solution)/shard_map/all_gather | solution.py:242
Sparse Core Ops, SparseCore 0:
  27.7 75.5 reduce-scatter.8
  107.1 84.0 reduce-scatter.4
  268.2 73.2 reduce-scatter.10
  345.2 85.2 reduce-scatter.6
Sparse Core Ops, SparseCore 1:
  47.8 35.7 all-gather.7
  85.7 39.9 all-reduce.2
  127.7 69.7 all-gather.11
  199.7 50.0 all-gather.5
  336.7 40.2 all-reduce.4
  379.1 58.0 all-gather.13
  439.3 49.7 all-gather.9

commit v2 on v1

v2 whole, which is shorter than its diff:
```python
import functools

import jax
import jax.numpy as jnp
from jax import lax
from jax.experimental import pallas as pl
from jax.experimental.pallas import tpu as pltpu
from jax.sharding import PartitionSpec as P

LANES = 128
PAD = 4
GELU_A = 0.7978845608028654
GELU_B = 0.044715
GELU_S = (GELU_A * GELU_B) ** (1.0 / 3.0)
MESH = pl.DeviceIdType.MESH


def bit_reversed(count):
    bits = count.bit_length() - 1
    return [int(format(i, "b").zfill(bits)[::-1], 2) if bits else 0 for i in range(count)]


def mode_order(modes, owners):
    each = modes // owners
    return [o * each + j for o in bit_reversed(owners) for j in range(each)]


def local_tables(first, count, length, order):
    modes = len(order)
    positions = first + jnp.arange(count, dtype=jnp.int32)
    orders = jnp.array(order, dtype=jnp.int32)
    phase = orders[:, None] * positions[None, :] % length
    angle = 2.0 * jnp.pi * phase.astype(jnp.float32) / length
    factor = 1.0 / jnp.sqrt(jnp.float32(length))
    weight_two = jnp.where(orders == 0, 1.0, 2.0).astype(jnp.float32)[:, None]
    real, imag = jnp.cos(angle) * factor, -jnp.sin(angle) * factor
    forward = jnp.stack([real, imag], axis=1).reshape(2 * modes, count)
    inverse = jnp.stack([weight_two * real, weight_two * imag], axis=1)
    inverse = inverse.reshape(2 * modes, count)
    return forward.astype(jnp.bfloat16), inverse.astype(jnp.bfloat16)


def dot(left, right):
    return jnp.dot(left, right, preferred_element_type=jnp.float32)


def dot_nt(left, right):
    return lax.dot_general(
        left, right, (((1,), (1,)), ((), ())), preferred_element_type=jnp.float32
    )


class Exchange:
    def __init__(self, axis, size, send, full, recv, send_sem, recv_sem, mix):
        self.axis, self.size = axis, size
        self.bits = size.bit_length() - 1
        self.stages = 2 * self.bits
        self.send, self.full, self.recv = send, full, recv
        self.send_sem, self.recv_sem = send_sem, recv_sem
        self.mix = mix
        self.me = lax.axis_index(axis)

    def bit(self, s):
        return lax.rem(self.me // (1 << s), 2)

    def base(self, s):
        total = 0
        for b in range(s):
            total = total + self.bit(b) * (self.size >> (b + 1))
        return total

    def partner(self, s):
        return self.me + (1 - 2 * self.bit(s)) * (1 << s)

    def copy(self, stage, m):
        if stage < self.bits:
            half = self.size >> (stage + 1)
            start = self.base(stage) + (1 - self.bit(stage)) * half
            src = self.send.at[m, pl.ds(start, half)]
            dst = self.recv[stage].at[m]
            peer = self.partner(stage)
        else:
            s = self.stages - 1 - stage
            half = self.size >> (s + 1)
            src = self.full.at[m, pl.ds(self.base(s + 1), half)]
            dst = self.full.at[m, pl.ds(self.base(s + 1), half)]
            peer = self.partner(s)
        return pltpu.make_async_remote_copy(
            src_ref=src,
            dst_ref=dst,
            send_sem=self.send_sem.at[stage, m],
            recv_sem=self.recv_sem.at[stage, m],
            device_id={self.axis: peer},
            device_id_type=MESH,
        )

    def start(self, stage, m):
        self.copy(stage, m).start()

    def finish(self, stage, layer, m):
        self.copy(stage, m).wait()
        if stage < self.bits:
            half = self.size >> (stage + 1)
            keep = self.base(stage + 1)
            rows = self.send.shape[2]
            got = self.recv[stage]

            @pl.loop(0, half)
            def _(i):
                for r in range(rows):
                    self.send[m, keep + i, r] = self.send[m, keep + i, r] + got[m, i, r]

            if stage == self.bits - 1:
                self.mix(layer, m, self.base(self.bits))
        if stage + 1 < self.stages:
            self.start(stage + 1, m)


def mega(layers, gx, gy, state_ref, fx_ref, fy_ref, ixt_ref, iy_ref, matx_ref, maty_ref,
         w1_ref, w2_ref, out_ref, *scratch):
    scratch = list(scratch)
    st, sx, mx, sy, my, t_ref, m_ref, acc_ref, a_ref = scratch[:9]
    bits_x, bits_y = gx.bit_length() - 1, gy.bit_length() - 1
    rx = scratch[9 : 9 + bits_x]
    ry = scratch[9 + bits_x : 9 + bits_x + bits_y]
    sendx, recvx, sendy, recvy, load_sem, store_sem = scratch[9 + bits_x + bits_y :]
    chunks, channels, rows, _ = st.shape
    rows2 = fx_ref.shape[0]
    per_x, per_y = rows2 // gx, rows2 // gy
    t_step, m_step = rows + PAD, channels + PAD
    bf16, f32 = jnp.bfloat16, jnp.float32

    def mix_x(layer, m, at):
        for j in range(per_x // 2):
            pair = sx[m, at, 2 * j : 2 * j + 2].reshape(2 * channels, LANES)
            got = dot(matx_ref[layer, j], pair).astype(bf16)
            mx[m, at, 2 * j : 2 * j + 2] = got.reshape(2, channels, LANES)

    def mix_y(layer, m, at):
        @pl.loop(0, per_y // 2)
        def _(j):
            pair = sy[m, at, pl.ds(2 * j, 2)].reshape(2 * channels, rows)
            got = dot(maty_ref[layer, j], pair).astype(bf16)
            my[m, at, pl.ds(2 * j, 2)] = got.reshape(2, channels, rows)

    ex = Exchange("gx", gx, sx, mx, rx, sendx, recvx, mix_x)
    ey = Exchange("gy", gy, sy, my, ry, sendy, recvy, mix_y)

    def lanes(m):
        return pl.ds(pl.multiple_of(m * LANES, LANES), LANES)

    def load(m):
        return pltpu.make_async_copy(state_ref.at[:, :, lanes(m)], st.at[m], load_sem.at[m])

    def store(m):
        return pltpu.make_async_copy(st.at[m], out_ref.at[:, :, lanes(m)], store_sem.at[m])

    def spectra(base, news, fx, fy):
        count = len(news)
        wide = dot(fx, jnp.concatenate(news, axis=1))
        tall = dot_nt(fy, jnp.concatenate(news, axis=0))
        for i in range(count):
            at = pl.ds((base + i) * m_step, rows2)
            m_ref[at, :] = wide[:, i * LANES : (i + 1) * LANES]
            acc_ref[at, :] = acc_ref[at, :] + tall[:, i * rows : (i + 1) * rows]

    def clear(m):
        @pl.when(m == 0)
        def _():
            acc_ref[...] = jnp.zeros_like(acc_ref)

    def send_spectra(m):
        for p in range(gx):
            for r in range(per_x):
                k = p * per_x + r
                sx[m, p, r] = m_ref[pl.ds(k, channels, stride=m_step), :].astype(bf16)
        ex.start(0, m)

        @pl.when(m == chunks - 1)
        def _():
            for p in range(gy):
                for r in range(per_y):
                    k = p * per_y + r
                    sy[0, p, r] = acc_ref[pl.ds(k, channels, stride=m_step), :].astype(bf16)
            if bits_y:
                ey.start(0, 0)

    def first_task(m):
        load(m).wait()
        clear(m)
        fx, fy = fx_ref[...], fy_ref[m]

        @pl.loop(0, channels // 4)
        def _(g):
            base = g * 4
            spectra(base, [st[m, base + i] for i in range(4)], fx, fy)

        send_spectra(m)

    def build_a():
        for p in range(gy):
            for r in range(per_y):
                at = pl.ds((p * per_y + r) * m_step, channels)
                acc_ref[at, :] = my[0, p, r].astype(f32)
        top = ixt_ref[...]

        @pl.loop(0, channels)
        def _(c):
            low = acc_ref[pl.ds(c, rows2, stride=m_step), :]
            a_ref[c] = jnp.concatenate([top, low], axis=0).T.astype(bf16)

    def layer_task(layer, m):
        for p in range(gx):
            for r in range(per_x):
                at = pl.ds((p * per_x + r) * m_step, channels)
                m_ref[at, :] = mx[m, p, r].astype(f32)
        iy = iy_ref[m]

        @pl.loop(0, channels // 4)
        def _(g):
            for i in range(4):
                c = g * 4 + i
                part = m_ref[pl.ds(c, rows2, stride=m_step), :].astype(bf16)
                t_ref[pl.ds(c * t_step, rows), :] = dot(
                    a_ref[c], jnp.concatenate([part, iy], axis=0)
                )

        w1, w2 = w1_ref[layer], w2_ref[layer]
        cg = jnp.bfloat16(GELU_A / GELU_S)

        @pl.loop(0, rows // 8)
        def _(g):
            base = g * 8
            parts = [t_ref[pl.ds(base + i, channels, stride=t_step), :] for i in range(8)]
            h = dot(w1, jnp.concatenate(parts, axis=1).astype(bf16)).astype(bf16)
            u = dot(w2, h + h * jnp.tanh(h * (h * h + cg)))
            for i in range(8):
                t_ref[pl.ds(base + i, channels, stride=t_step), :] = u[
                    :, i * LANES : (i + 1) * LANES
                ]

        def updated(c):
            new = st[m, c].astype(f32) + t_ref[pl.ds(c * t_step, rows), :]
            new = new.astype(bf16)
            st[m, c] = new
            return new

        @pl.when(layer < layers - 1)
        def _():
            clear(m)
            fx, fy = fx_ref[...], fy_ref[m]

            @pl.loop(0, channels // 4)
            def _(g):
                base = g * 4
                spectra(base, [updated(base + i) for i in range(4)], fx, fy)

            send_spectra(m)

        @pl.when(layer == layers - 1)
        def _():
            @pl.loop(0, channels // 4)
            def _(g):
                for i in range(4):
                    updated(g * 4 + i)

            store(m).start()

    barrier = pltpu.get_barrier_semaphore()
    for one in (ex, ey):
        for s in range(one.bits):
            pl.semaphore_signal(
                barrier, inc=1, device_id={one.axis: one.partner(s)}, device_id_type=MESH
            )

    @pl.loop(0, chunks)
    def _(m):
        load(m).start()

    pl.semaphore_wait(barrier, ex.bits + ey.bits)

    period = max(chunks + 1, ex.stages + 1, chunks - 1 + ey.stages)
    ticks = layers * period + chunks

    @pl.loop(0, ticks)
    def _(t):
        for stage in reversed(range(ey.stages)):
            q = t - chunks - stage
            layer = q // period

            @pl.when((q >= 0) & (lax.rem(q, period) == 0) & (layer < layers))
            def _():
                ey.finish(stage, layer, 0)

        for stage in reversed(range(ex.stages)):
            q = t - 1 - stage
            layer = q // period
            m = lax.rem(q, period)

            @pl.when((q >= 0) & (m < chunks) & (layer < layers))
            def _():
                ex.finish(stage, layer, m)

        turn = t // period
        m = lax.rem(t, period)

        @pl.when(t < chunks)
        def _():
            first_task(m)

        @pl.when((turn > 0) & (m == 0))
        def _():
            build_a()

        @pl.when((turn > 0) & (m < chunks))
        def _():
            layer_task(turn - 1, m)

    @pl.loop(0, chunks)
    def _(m):
        store(m).wait()


def body(state_field, spectral_x, spectral_y, expand_weight, reduce_weight):
    planes, channels, rows, cols = state_field.shape
    layers, hidden = expand_weight.shape[0], expand_weight.shape[2]
    gx, gy = lax.axis_size("gx"), lax.axis_size("gy")
    nx, ny = rows * gx, cols * gy
    modes = spectral_x.shape[1] * gx
    rows2 = 2 * modes
    chunks = cols // LANES
    bf16, f32 = jnp.bfloat16, jnp.float32
    forward_x, inverse_x = local_tables(
        lax.axis_index("gx") * rows, rows, nx, mode_order(modes, gx)
    )
    forward_y, inverse_y = local_tables(
        lax.axis_index("gy") * cols, cols, ny, mode_order(modes, gy)
    )

    def by_chunk(table):
        return jnp.transpose(table.reshape(rows2, chunks, LANES), (1, 0, 2))

    def block_matrix(w):
        top = jnp.concatenate([w[..., 0, :, :], -w[..., 1, :, :]], axis=-1)
        low = jnp.concatenate([w[..., 1, :, :], w[..., 0, :, :]], axis=-1)
        return jnp.concatenate([top, low], axis=-2)

    w1 = jnp.swapaxes((expand_weight.astype(f32) * GELU_S).astype(bf16), 1, 2)
    w2 = jnp.swapaxes((reduce_weight.astype(f32) * (0.5 / GELU_S)).astype(bf16), 1, 2)
    args = [
        state_field.reshape(channels, rows, cols),
        forward_x,
        by_chunk(forward_y),
        inverse_x.astype(f32),
        by_chunk(inverse_y),
        block_matrix(spectral_x),
        block_matrix(spectral_y),
        w1,
        w2,
    ]
    bits_x, bits_y = gx.bit_length() - 1, gy.bit_length() - 1
    per_x, per_y = rows2 // gx, rows2 // gy
    m_rows = max(channels, rows2) * (max(channels, rows2) + PAD)
    scratch = [
        pltpu.VMEM((chunks, channels, rows, LANES), bf16),
        pltpu.VMEM((chunks, gx, per_x, channels, LANES), bf16),
        pltpu.VMEM((chunks, gx, per_x, channels, LANES), bf16),
        pltpu.VMEM((1, gy, per_y, channels, rows), bf16),
        pltpu.VMEM((1, gy, per_y, channels, rows), bf16),
        pltpu.VMEM((channels * (rows + PAD), LANES), f32),
        pltpu.VMEM((m_rows, LANES), f32),
        pltpu.VMEM((m_rows, rows), f32),
        pltpu.VMEM((channels, rows, 2 * rows2), bf16),
    ]
    for s in range(bits_x):
        scratch.append(pltpu.VMEM((chunks, gx >> (s + 1), per_x, channels, LANES), bf16))
    for s in range(bits_y):
        scratch.append(pltpu.VMEM((1, gy >> (s + 1), per_y, channels, rows), bf16))
    dma = pltpu.SemaphoreType.DMA
    scratch += [dma((2 * bits_x, chunks))] * 2 + [dma((2 * bits_y, 1))] * 2 + [dma((chunks,))] * 2
    vmem = pl.BlockSpec(memory_space=pltpu.VMEM)
    anywhere = pl.BlockSpec(memory_space=pl.ANY)
    out = pl.pallas_call(
        functools.partial(mega, layers, gx, gy),
        name="layers",
        out_shape=jax.ShapeDtypeStruct((channels, rows, cols), bf16),
        in_specs=[anywhere] + [vmem] * (len(args) - 1),
        out_specs=anywhere,
        scratch_shapes=scratch,
        compiler_params=pltpu.CompilerParams(
            collective_id=0, has_side_effects=True, vmem_limit_bytes=67043328
        ),
    )(*args)
    return out.reshape(state_field.shape)


def solution(mesh):
    in_specs = (
        P(None, None, "gx", "gy"),
        P(None, "gx", None, None, None),
        P(None, "gy", None, None, None),
        P(),
        P(),
    )
    out_specs = P(None, None, "gx", "gy")
    return jax.shard_map(body, mesh=mesh, in_specs=in_specs, out_specs=out_specs, check_vma=False)
```

time: 543 us -> 365 us (0.67)
  waiting for transfers between devices: 229 us -> 0 us
  Pallas kernels: 248 us -> 340 us
  between operations: 14.9 us -> 0.1 us
  other arithmetic: 19.9 us -> 6.91 us
  matrix products: 11.9 us -> 0 us
    reduce_scatter x4 -> x0, waiting for transfers between devices: 227 us -> none  [body(): lax.psum_scatter(s, 'gx', scatter_dimension=0, tiled=True)]
    pallas_call x6 -> x1, Pallas kernels: 248 us -> 340 us  [body(): pl.pallas_call(functools.partial(mega, layers, gx, gy), name='layers', ou...]
    dot_general x6 -> x0, matrix products: 11.9 us -> none  [the longest x4 7.52 us: body(): jnp.einsum('moi,miy->moy', mat_x[layer], pairs, preferred_element_type=jn...]
    unnamed x17 -> x5, local copies, waits for them, and re-layouts: 4.05 us -> 13.9 us
    transpose x5 -> x2, other arithmetic: 9.77 us -> 2.15 us  [the longest x1 1.47 us: body(): jnp.swapaxes((reduce_weight.astype(f32) * (0.5 / GELU_S)).astype(bf16), 1...]
    concatenate x2 -> x0, other arithmetic: 6.58 us -> none  [body(): jnp.concatenate([jnp.broadcast_to(inverse_xt[None], (channels, rows, rows...]
    transpose x3 -> x0, local copies, waits for them, and re-layouts: 6.02 us -> none  [the longest x2 5.91 us: body(): spec_y = lax.psum(jnp.transpose(spec_y, (2, 0, 1)), 'gy')]
  transfers between devices with their start and end apart: 11 -> 0, of which waited for: 5 -> 0; matrix products, arithmetic and copies ran while one was open for 8% -> 0% of each run, Pallas kernels for 34% -> 0%
where the time goes in v2:
time: 365 us
  Pallas kernels  340 us (93%)
  local copies, waits for them, and re-layouts  18 us (5%)
  other arithmetic  6.91 us (2%)
    pallas_call x1, Pallas kernels, body(): pl.pallas_call(functools.partial(mega, layers, gx, gy), name='layers', ou...  340 us
    unnamed x5, local copies, waits for them, and re-layouts  13.9 us

profile of v2, /device:TPU:0, one launch (start us, length us, event | category | flops | bytes accessed | tf_op | source)
XLA Modules:
  0.0 364.6 jit_solution(7228158084905196198)
XLA Ops:
  0.0 0.0 copy-start.1
  0.0 0.0 copy-start
  0.0 0.9 multiply_convert_fusion.7
  1.0 0.6 copy.20
  1.6 0.6 copy.23
  2.2 1.5 fusion.7.w2_ref
  3.7 0.8 fusion.14
  4.5 0.9 slice_bitcast_fusion.2
  5.4 0.8 maximum_maximum_fusion.1.matx_ref
  6.2 0.6 multiply_convert_fusion.3
  6.8 0.1 copy.21
  6.9 0.1 convert_element_type.79
  7.0 0.7 copy.38
  7.7 0.1 copy.24
  7.8 0.1 convert_element_type.82
  7.9 0.7 copy.37
  8.6 0.0 copy-done.1
  8.6 0.1 copy.30
  8.7 0.7 fusion.3.w1_ref
  9.4 0.0 copy-done
  9.4 0.1 fusion.15
  9.5 0.1 slice_bitcast_fusion
  9.6 1.6 maximum_maximum_fusion.maty_ref
  11.1 339.6 %layers.1 = bf16[64,128,1024]{2,1,0:T(8,128)(2,1)} custom-call(bf16[64,128,1024]{2,1,0:T(8,128)(2,1)} %bitcast.35, bf16[64,128]{1,0:T(8,128)(2,1)} %bitcast.39, bf16[8,64,128]{2,1,0:T(8,128)(2,1)} %bitcast.36, f32[64,128]{1,0:T(8,128)} %bitcast.38, bf16[8,64,128]{2,1,0:T(8,128)(2,1)} %bitcast.37, bf16[2,2,128,128]{3,2,1,0:T(8,128)(2,1)} %maximum_maximum_fusion.1.matx_ref, ...), custom_call_target="tpu_custom_call" | custom-call | tf_op jit(solution)/shard_map/layers/pallas_call | solution.py:383
  350.7 13.9 %copy.40 = bf16[1,64,128,1024]{3,2,1,0:T(8,128)(2,1)} copy(bf16[1,64,128,1024]{3,2,1,0:T(8,128)(2,1)} %bitcast.34) | data formatting | bytes 33554432
  (5 shorter events, 0.0 us)
Async XLA Ops:
  0.0 8.6 %copy-start.1 = (bf16[2,64,256]{2,1,0:T(8,128)(2,1)S(1)}, bf16[2,64,256]{2,1,0:T(8,128)(2,1)}, u32[]{:S(2)}) copy-start(bf16[2,64,256]{2,1,0:T(8,128)(2,1)} %param.10) | copy-start | bytes 196612
  0.0 9.4 %copy-start = (bf16[2,16,2,64,64]{4,3,2,1,0:T(8,128)(2,1)S(1)}, bf16[2,16,2,64,64]{4,3,2,1,0:T(8,128)(2,1)}, u32[]{:S(2)}) copy-start(bf16[2,16,2,64,64]{4,3,2,1,0:T(8,128)(2,1)} %param.9) | copy-start | bytes 1572868

commit v3 on v2

--- a/solution.py
+++ b/solution.py
@@ -9,6 +9,8 @@
 
 LANES = 128
 PAD = 4
+GROUP = 8
+WIDE = 16
 GELU_A = 0.7978845608028654
 GELU_B = 0.044715
 GELU_S = (GELU_A * GELU_B) ** (1.0 / 3.0)
@@ -48,6 +50,13 @@
     return lax.dot_general(
         left, right, (((1,), (1,)), ((), ())), preferred_element_type=jnp.float32
     )
+
+
+def stage_order(stages):
+    first = [0, stages - 3] if stages >= 4 else []
+    last = [1, stages - 2] if stages >= 4 else []
+    middle = [s for s in reversed(range(stages)) if s not in first + last]
+    return list(dict.fromkeys(first + middle + last))
 
 
 class Exchange:
@@ -119,11 +128,11 @@
 def mega(layers, gx, gy, state_ref, fx_ref, fy_ref, ixt_ref, iy_ref, matx_ref, maty_ref,
          w1_ref, w2_ref, out_ref, *scratch):
     scratch = list(scratch)
-    st, sx, mx, sy, my, t_ref, m_ref, acc_ref, a_ref = scratch[:9]
+    st, sx, mx, sy, my, t_ref, u_ref, h0_ref, h1_ref, m_ref, acc_ref, a_ref = scratch[:12]
     bits_x, bits_y = gx.bit_length() - 1, gy.bit_length() - 1
-    rx = scratch[9 : 9 + bits_x]
-    ry = scratch[9 + bits_x : 9 + bits_x + bits_y]
-    sendx, recvx, sendy, recvy, load_sem, store_sem = scratch[9 + bits_x + bits_y :]
+    rx = scratch[12 : 12 + bits_x]
+    ry = scratch[12 + bits_x : 12 + bits_x + bits_y]
+    sendx, recvx, sendy, recvy, load_sem, store_sem = scratch[12 + bits_x + bits_y :]
     chunks, channels, rows, _ = st.shape
     rows2 = fx_ref.shape[0]
     per_x, per_y = rows2 // gx, rows2 // gy
@@ -190,10 +199,10 @@
         clear(m)
         fx, fy = fx_ref[...], fy_ref[m]
 
-        @pl.loop(0, channels // 4)
+        @pl.loop(0, channels // WIDE)
         def _(g):
-            base = g * 4
-            spectra(base, [st[m, base + i] for i in range(4)], fx, fy)
+            base = g * WIDE
+            spectra(base, [st[m, base + i] for i in range(WIDE)], fx, fy)
 
         send_spectra(m)
 
@@ -216,10 +225,10 @@
                 m_ref[at, :] = mx[m, p, r].astype(f32)
         iy = iy_ref[m]
 
-        @pl.loop(0, channels // 4)
+        @pl.loop(0, channels // WIDE)
         def _(g):
-            for i in range(4):
-                c = g * 4 + i
+            for i in range(WIDE):
+                c = g * WIDE + i
                 part = m_ref[pl.ds(c, rows2, stride=m_step), :].astype(bf16)
                 t_ref[pl.ds(c * t_step, rows), :] = dot(
                     a_ref[c], jnp.concatenate([part, iy], axis=0)
@@ -228,19 +237,30 @@
         w1, w2 = w1_ref[layer], w2_ref[layer]
         cg = jnp.bfloat16(GELU_A / GELU_S)
 
-        @pl.loop(0, rows // 8)
-        def _(g):
-            base = g * 8
-            parts = [t_ref[pl.ds(base + i, channels, stride=t_step), :] for i in range(8)]
-            h = dot(w1, jnp.concatenate(parts, axis=1).astype(bf16)).astype(bf16)
+        def expand(base, h_ref):
+            parts = [t_ref[pl.ds(base + i, channels, stride=t_step), :] for i in range(GROUP)]
+            h_ref[...] = dot(w1, jnp.concatenate(parts, axis=1).astype(bf16)).astype(bf16)
+
+        def reduce(base, h_ref):
+            h = h_ref[...]
             u = dot(w2, h + h * jnp.tanh(h * (h * h + cg)))
-            for i in range(8):
-                t_ref[pl.ds(base + i, channels, stride=t_step), :] = u[
+            for i in range(GROUP):
+                u_ref[pl.ds(base + i, channels, stride=t_step), :] = u[
                     :, i * LANES : (i + 1) * LANES
                 ]
 
+        expand(0, h0_ref)
+
+        @pl.loop(0, rows // (2 * GROUP))
+        def _(g):
+            base = g * 2 * GROUP
+            expand(base + GROUP, h1_ref)
+            reduce(base, h0_ref)
+            expand(lax.rem(base + 2 * GROUP, rows), h0_ref)
+            reduce(base + GROUP, h1_ref)
+
         def updated(c):
-            new = st[m, c].astype(f32) + t_ref[pl.ds(c * t_step, rows), :]
+            new = st[m, c].astype(f32) + u_ref[pl.ds(c * t_step, rows), :]
             new = new.astype(bf16)
             st[m, c] = new
             return new
@@ -250,10 +270,10 @@
             clear(m)
             fx, fy = fx_ref[...], fy_ref[m]
 
-            @pl.loop(0, channels // 4)
+            @pl.loop(0, channels // WIDE)
             def _(g):
-                base = g * 4
-                spectra(base, [updated(base + i) for i in range(4)], fx, fy)
+                base = g * WIDE
+                spectra(base, [updated(base + i) for i in range(WIDE)], fx, fy)
 
             send_spectra(m)
 
@@ -292,7 +312,7 @@
             def _():
                 ey.finish(stage, layer, 0)
 
-        for stage in reversed(range(ex.stages)):
+        for stage in stage_order(ex.stages):
             q = t - 1 - stage
             layer = q // period
             m = lax.rem(q, period)
@@ -368,6 +388,9 @@
         pltpu.VMEM((1, gy, per_y, channels, rows), bf16),
         pltpu.VMEM((1, gy, per_y, channels, rows), bf16),
         pltpu.VMEM((channels * (rows + PAD), LANES), f32),
+        pltpu.VMEM((channels * (rows + PAD), LANES), f32),
+        pltpu.VMEM((hidden, GROUP * LANES), bf16),
+        pltpu.VMEM((hidden, GROUP * LANES), bf16),
         pltpu.VMEM((m_rows, LANES), f32),
         pltpu.VMEM((m_rows, rows), f32),
         pltpu.VMEM((channels, rows, 2 * rows2), bf16),

time: 365 us -> 299 us (0.82)
  Pallas kernels: 340 us -> 274 us
    pallas_call x1, Pallas kernels: 340 us -> 274 us  [body(): pl.pallas_call(functools.partial(mega, layers, gx, gy), name='layers', ou...]
where the time goes in v3:
time: 299 us
  Pallas kernels  274 us (92%)
  local copies, waits for them, and re-layouts  18 us (6%)
  other arithmetic  6.91 us (2%)
    pallas_call x1, Pallas kernels, body(): pl.pallas_call(functools.partial(mega, layers, gx, gy), name='layers', ou...  274 us
    unnamed x5, local copies, waits for them, and re-layouts  13.9 us

profile of v3, /device:TPU:0, one launch (start us, length us, event | category | flops | bytes accessed | tf_op | source)
XLA Modules:
  0.0 298.5 jit_solution(15698558081493533207)
XLA Ops:
  0.0 0.0 copy-start.1
  0.0 0.0 copy-start
  0.0 0.9 multiply_convert_fusion.7
  1.0 0.6 copy.20
  1.6 0.6 copy.23
  2.2 1.5 fusion.7.w2_ref
  3.7 0.8 fusion.14
  4.5 0.9 slice_bitcast_fusion.2
  5.4 0.8 maximum_maximum_fusion.1.matx_ref
  6.2 0.6 multiply_convert_fusion.3
  6.8 0.1 copy.21
  6.9 0.1 convert_element_type.79
  7.0 0.7 copy.38
  7.7 0.1 copy.24
  7.8 0.1 convert_element_type.82
  7.9 0.7 copy.37
  8.6 0.0 copy-done.1
  8.6 0.1 copy.30
  8.7 0.7 fusion.3.w1_ref
  9.4 0.0 copy-done
  9.4 0.1 fusion.15
  9.5 0.1 slice_bitcast_fusion
  9.6 1.6 maximum_maximum_fusion.maty_ref
  11.1 273.5 %layers.1 = bf16[64,128,1024]{2,1,0:T(8,128)(2,1)} custom-call(bf16[64,128,1024]{2,1,0:T(8,128)(2,1)} %bitcast.35, bf16[64,128]{1,0:T(8,128)(2,1)} %bitcast.39, bf16[8,64,128]{2,1,0:T(8,128)(2,1)} %bitcast.36, f32[64,128]{1,0:T(8,128)} %bitcast.38, bf16[8,64,128]{2,1,0:T(8,128)(2,1)} %bitcast.37, bf16[2,2,128,128]{3,2,1,0:T(8,128)(2,1)} %maximum_maximum_fusion.1.matx_ref, ...), custom_call_target="tpu_custom_call" | custom-call | tf_op jit(solution)/shard_map/layers/pallas_call | solution.py:406
  284.6 13.9 %copy.40 = bf16[1,64,128,1024]{3,2,1,0:T(8,128)(2,1)} copy(bf16[1,64,128,1024]{3,2,1,0:T(8,128)(2,1)} %bitcast.34) | data formatting | bytes 33554432
  (5 shorter events, 0.0 us)
Async XLA Ops:
  0.0 8.6 %copy-start.1 = (bf16[2,64,256]{2,1,0:T(8,128)(2,1)S(1)}, bf16[2,64,256]{2,1,0:T(8,128)(2,1)}, u32[]{:S(2)}) copy-start(bf16[2,64,256]{2,1,0:T(8,128)(2,1)} %param.10) | copy-start | bytes 196612
  0.0 9.4 %copy-start = (bf16[2,16,2,64,64]{4,3,2,1,0:T(8,128)(2,1)S(1)}, bf16[2,16,2,64,64]{4,3,2,1,0:T(8,128)(2,1)}, u32[]{:S(2)}) copy-start(bf16[2,16,2,64,64]{4,3,2,1,0:T(8,128)(2,1)} %param.9) | copy-start | bytes 1572868

commit v4 on v3

--- a/solution.py
+++ b/solution.py
@@ -28,17 +28,14 @@
 
 
 def local_tables(first, count, length, order):
-    modes = len(order)
+    rows2 = 2 * len(order)
     positions = first + jnp.arange(count, dtype=jnp.int32)
-    orders = jnp.array(order, dtype=jnp.int32)
-    phase = orders[:, None] * positions[None, :] % length
-    angle = 2.0 * jnp.pi * phase.astype(jnp.float32) / length
+    orders = jnp.array([k for k in order for _ in range(2)], dtype=jnp.int32)[:, None]
+    part = lax.broadcasted_iota(jnp.int32, (rows2, count), 0) % 2
+    angle = 2.0 * jnp.pi * (orders * positions[None, :] % length).astype(jnp.float32) / length
     factor = 1.0 / jnp.sqrt(jnp.float32(length))
-    weight_two = jnp.where(orders == 0, 1.0, 2.0).astype(jnp.float32)[:, None]
-    real, imag = jnp.cos(angle) * factor, -jnp.sin(angle) * factor
-    forward = jnp.stack([real, imag], axis=1).reshape(2 * modes, count)
-    inverse = jnp.stack([weight_two * real, weight_two * imag], axis=1)
-    inverse = inverse.reshape(2 * modes, count)
+    forward = jnp.where(part == 0, jnp.cos(angle), -jnp.sin(angle)) * factor
+    inverse = jnp.where(orders == 0, 1.0, 2.0) * forward
     return forward.astype(jnp.bfloat16), inverse.astype(jnp.bfloat16)
 
 
@@ -54,9 +51,9 @@
 
 def stage_order(stages):
     first = [0, stages - 3] if stages >= 4 else []
-    last = [1, stages - 2] if stages >= 4 else []
-    middle = [s for s in reversed(range(stages)) if s not in first + last]
-    return list(dict.fromkeys(first + middle + last))
+    late = [1, stages - 2] if stages >= 4 else []
+    middle = [s for s in reversed(range(stages - 1)) if s not in first + late]
+    return list(dict.fromkeys(first + middle + late)) + [stages - 1]
 
 
 class Exchange:
@@ -125,14 +122,15 @@
             self.start(stage + 1, m)
 
 
-def mega(layers, gx, gy, state_ref, fx_ref, fy_ref, ixt_ref, iy_ref, matx_ref, maty_ref,
-         w1_ref, w2_ref, out_ref, *scratch):
+def mega(layers, gx, gy, state_ref, fx_ref, fy_ref, ixt_ref, iy_ref, spx_ref, spy_ref,
+         ew_ref, rw_ref, out_ref, *scratch):
     scratch = list(scratch)
     st, sx, mx, sy, my, t_ref, u_ref, h0_ref, h1_ref, m_ref, acc_ref, a_ref = scratch[:12]
+    matx_ref, maty_ref, w1_ref, w2_ref = scratch[12:16]
     bits_x, bits_y = gx.bit_length() - 1, gy.bit_length() - 1
-    rx = scratch[12 : 12 + bits_x]
-    ry = scratch[12 + bits_x : 12 + bits_x + bits_y]
-    sendx, recvx, sendy, recvy, load_sem, store_sem = scratch[12 + bits_x + bits_y :]
+    rx = scratch[16 : 16 + bits_x]
+    ry = scratch[16 + bits_x : 16 + bits_x + bits_y]
+    sendx, recvx, sendy, recvy, load_sem, store_sem = scratch[16 + bits_x + bits_y :]
     chunks, channels, rows, _ = st.shape
     rows2 = fx_ref.shape[0]
     per_x, per_y = rows2 // gx, rows2 // gy
@@ -154,6 +152,18 @@
 
     ex = Exchange("gx", gx, sx, mx, rx, sendx, recvx, mix_x)
     ey = Exchange("gy", gy, sy, my, ry, sendy, recvy, mix_y)
+
+    def prepare():
+        for layer in range(layers):
+            w1_ref[layer] = (ew_ref[layer].astype(f32) * GELU_S).T.astype(bf16)
+            w2_ref[layer] = (rw_ref[layer].astype(f32) * (0.5 / GELU_S)).T.astype(bf16)
+            for source, target in ((spx_ref, matx_ref), (spy_ref, maty_ref)):
+
+                @pl.loop(0, source.shape[1])
+                def _(j):
+                    real, imag = source[layer, j, 0], source[layer, j, 1]
+                    target[layer, j, :channels] = jnp.concatenate([real, -imag], axis=1)
+                    target[layer, j, channels:] = jnp.concatenate([imag, real], axis=1)
 
     def lanes(m):
         return pl.ds(pl.multiple_of(m * LANES, LANES), LANES)
@@ -197,7 +207,7 @@
     def first_task(m):
         load(m).wait()
         clear(m)
-        fx, fy = fx_ref[...], fy_ref[m]
+        fx, fy = fx_ref[...], fy_ref[:, lanes(m)]
 
         @pl.loop(0, channels // WIDE)
         def _(g):
@@ -211,19 +221,20 @@
             for r in range(per_y):
                 at = pl.ds((p * per_y + r) * m_step, channels)
                 acc_ref[at, :] = my[0, p, r].astype(f32)
-        top = ixt_ref[...]
-
-        @pl.loop(0, channels)
-        def _(c):
-            low = acc_ref[pl.ds(c, rows2, stride=m_step), :]
-            a_ref[c] = jnp.concatenate([top, low], axis=0).T.astype(bf16)
-
-    def layer_task(layer, m):
+        top = ixt_ref[...].astype(f32)
+
+        @pl.loop(0, channels // 8)
+        def _(g):
+            for i in range(8):
+                low = acc_ref[pl.ds(g * 8 + i, rows2, stride=m_step), :]
+                a_ref[g * 8 + i] = jnp.concatenate([top, low], axis=0).T.astype(bf16)
+
+    def layer_start(m):
         for p in range(gx):
             for r in range(per_x):
                 at = pl.ds((p * per_x + r) * m_step, channels)
                 m_ref[at, :] = mx[m, p, r].astype(f32)
-        iy = iy_ref[m]
+        iy = iy_ref[:, lanes(m)]
 
         @pl.loop(0, channels // WIDE)
         def _(g):
@@ -234,6 +245,7 @@
                     a_ref[c], jnp.concatenate([part, iy], axis=0)
                 )
 
+    def layer_rest(layer, m):
         w1, w2 = w1_ref[layer], w2_ref[layer]
         cg = jnp.bfloat16(GELU_A / GELU_S)
 
@@ -268,7 +280,7 @@
         @pl.when(layer < layers - 1)
         def _():
             clear(m)
-            fx, fy = fx_ref[...], fy_ref[m]
+            fx, fy = fx_ref[...], fy_ref[:, lanes(m)]
 
             @pl.loop(0, channels // WIDE)
             def _(g):
@@ -299,34 +311,35 @@
 
     pl.semaphore_wait(barrier, ex.bits + ey.bits)
 
-    period = max(chunks + 1, ex.stages + 1, chunks - 1 + ey.stages)
-    ticks = layers * period + chunks
-
-    @pl.loop(0, ticks)
+    prepare()
+    early = pl.cdiv(chunks, 2)
+    period = max(chunks, ex.stages, early + 1 + ey.stages)
+
+    @pl.loop(0, layers * period + chunks)
     def _(t):
-        for stage in reversed(range(ey.stages)):
-            q = t - chunks - stage
-            layer = q // period
-
-            @pl.when((q >= 0) & (lax.rem(q, period) == 0) & (layer < layers))
+        turn, m = t // period, lax.rem(t, period)
+
+        def advance(stage):
+            q = t - 1 - stage
+            layer, chunk = q // period, lax.rem(q, period)
+
+            @pl.when((q >= 0) & (chunk < chunks) & (layer < layers))
             def _():
-                ey.finish(stage, layer, 0)
-
-        for stage in stage_order(ex.stages):
-            q = t - 1 - stage
-            layer = q // period
-            m = lax.rem(q, period)
-
-            @pl.when((q >= 0) & (m < chunks) & (layer < layers))
+                ex.finish(stage, layer, chunk)
+
+        if ex.stages:
+            advance(ex.stages - 1)
+        for stage in range(ey.stages):
+
+            @pl.when((t == early + 1 + stage) | ((turn > 1) & (m == 0)))
             def _():
-                ex.finish(stage, layer, m)
-
-        turn = t // period
-        m = lax.rem(t, period)
-
-        @pl.when(t < chunks)
-        def _():
-            first_task(m)
+                ey.finish(stage, jnp.maximum(turn - 1, 0), 0)
+
+        for i in range(2):
+
+            @pl.when(2 * t + i < chunks)
+            def _():
+                first_task(2 * t + i)
 
         @pl.when((turn > 0) & (m == 0))
         def _():
@@ -334,7 +347,14 @@
 
         @pl.when((turn > 0) & (m < chunks))
         def _():
-            layer_task(turn - 1, m)
+            layer_start(m)
+
+        for stage in stage_order(ex.stages)[:-1] if ex.stages else []:
+            advance(stage)
+
+        @pl.when((turn > 0) & (m < chunks))
+        def _():
+            layer_rest(turn - 1, m)
 
     @pl.loop(0, chunks)
     def _(m):
@@ -350,6 +370,8 @@
     rows2 = 2 * modes
     chunks = cols // LANES
     bf16, f32 = jnp.bfloat16, jnp.float32
+    own_y = spectral_y.shape[1]
+    own_x = spectral_x.shape[1]
     forward_x, inverse_x = local_tables(
         lax.axis_index("gx") * rows, rows, nx, mode_order(modes, gx)
     )
@@ -357,26 +379,16 @@
         lax.axis_index("gy") * cols, cols, ny, mode_order(modes, gy)
     )
 
-    def by_chunk(table):
-        return jnp.transpose(table.reshape(rows2, chunks, LANES), (1, 0, 2))
-
-    def block_matrix(w):
-        top = jnp.concatenate([w[..., 0, :, :], -w[..., 1, :, :]], axis=-1)
-        low = jnp.concatenate([w[..., 1, :, :], w[..., 0, :, :]], axis=-1)
-        return jnp.concatenate([top, low], axis=-2)
-
-    w1 = jnp.swapaxes((expand_weight.astype(f32) * GELU_S).astype(bf16), 1, 2)
-    w2 = jnp.swapaxes((reduce_weight.astype(f32) * (0.5 / GELU_S)).astype(bf16), 1, 2)
     args = [
         state_field.reshape(channels, rows, cols),
         forward_x,
-        by_chunk(forward_y),
-        inverse_x.astype(f32),
-        by_chunk(inverse_y),
-        block_matrix(spectral_x),
-        block_matrix(spectral_y),
-        w1,
-        w2,
+        forward_y,
+        inverse_x,
+        inverse_y,
+        spectral_x,
+        spectral_y,
+        expand_weight,
+        reduce_weight,
     ]
     bits_x, bits_y = gx.bit_length() - 1, gy.bit_length() - 1
     per_x, per_y = rows2 // gx, rows2 // gy
@@ -394,6 +406,10 @@
         pltpu.VMEM((m_rows, LANES), f32),
         pltpu.VMEM((m_rows, rows), f32),
         pltpu.VMEM((channels, rows, 2 * rows2), bf16),
+        pltpu.VMEM((layers, own_x, 2 * channels, 2 * channels), bf16),
+        pltpu.VMEM((layers, own_y, 2 * channels, 2 * channels), bf16),
+        pltpu.VMEM((layers, hidden, channels), bf16),
+        pltpu.VMEM((layers, channels, hidden), bf16),
     ]
     for s in range(bits_x):
         scratch.append(pltpu.VMEM((chunks, gx >> (s + 1), per_x, channels, LANES), bf16))

time: 299 us -> 275 us (0.920)
  Pallas kernels: 274 us -> 255 us
    pallas_call x1, Pallas kernels: 274 us -> 255 us  [body(): pl.pallas_call(functools.partial(mega, layers, gx, gy), name='layers', ou...]
    convert_element_type x0 -> x2, other arithmetic: none -> 4.11 us  [local_tables(): return (forward.astype(jnp.bfloat16), inverse.astype(jnp.bfloat16))]
    unnamed x5 -> x2, local copies, waits for them, and re-layouts: 13.9 us -> 15.5 us
where the time goes in v4:
time: 275 us
  Pallas kernels  255 us (93%)
  local copies, waits for them, and re-layouts  15.5 us (6%)
  other arithmetic  4.13 us (2%)
    pallas_call x1, Pallas kernels, body(): pl.pallas_call(functools.partial(mega, layers, gx, gy), name='layers', ou...  255 us
    unnamed x2, local copies, waits for them, and re-layouts  15.5 us

profile of v4, /device:TPU:0, one launch (start us, length us, event | category | flops | bytes accessed | tf_op | source)
XLA Modules:
  0.0 274.6 jit_solution(15104998881687216513)
XLA Ops:
  0.0 1.5 multiply_convert_fusion.2
  1.5 1.6 copy.8.rw_ref
  3.1 2.6 multiply_convert_fusion
  5.7 255.0 %layers.1 = bf16[64,128,1024]{2,1,0:T(8,128)(2,1)} custom-call(bf16[64,128,1024]{2,1,0:T(8,128)(2,1)} %bitcast.3, bf16[64,128]{1,0:T(8,128)(2,1)} %get-tuple-element.8.fx_ref, bf16[64,1024]{1,0:T(8,128)(2,1)} %get-tuple-element.6.fy_ref, bf16[64,128]{1,0:T(8,128)(2,1)} %get-tuple-element.7.ixt_ref, bf16[64,1024]{1,0:T(8,128)(2,1)} %get-tuple-element.5.iy_ref, ...), custom_call_target="tpu_custom_call" | custom-call | tf_op jit(solution)/shard_map/layers/pallas_call | solution.py:422
  260.7 13.9 %copy.10 = bf16[1,64,128,1024]{3,2,1,0:T(8,128)(2,1)} copy(bf16[1,64,128,1024]{3,2,1,0:T(8,128)(2,1)} %bitcast.2) | data formatting | bytes 33554432
  (4 shorter events, 0.0 us)

commit v5 on v4

--- a/solution.py
+++ b/solution.py
@@ -122,15 +122,127 @@
             self.start(stage + 1, m)
 
 
-def mega(layers, gx, gy, state_ref, fx_ref, fy_ref, ixt_ref, iy_ref, spx_ref, spy_ref,
-         ew_ref, rw_ref, out_ref, *scratch):
+def transform(mixed_ref, a_ref, iy, m_ref, t_ref):
+    owners, each, channels, _ = mixed_ref.shape
+    rows, rows2 = a_ref.shape[1], owners * each
+    t_step, m_step = rows + PAD, channels + PAD
+    for p in range(owners):
+        for r in range(each):
+            at = pl.ds((p * each + r) * m_step, channels)
+            m_ref[at, :] = mixed_ref[p, r].astype(jnp.float32)
+
+    @pl.loop(0, channels // WIDE)
+    def _(g):
+        for i in range(WIDE):
+            c = g * WIDE + i
+            part = m_ref[pl.ds(c, rows2, stride=m_step), :].astype(jnp.bfloat16)
+            t_ref[pl.ds(c * t_step, rows), :] = dot(a_ref[c], jnp.concatenate([part, iy], axis=0))
+
+
+def pointwise(w1, w2, rows, t_ref, u_ref, h0_ref, h1_ref):
+    channels, t_step = w2.shape[0], rows + PAD
+    cg = jnp.bfloat16(GELU_A / GELU_S)
+
+    def expand(base, h_ref):
+        parts = [t_ref[pl.ds(base + i, channels, stride=t_step), :] for i in range(GROUP)]
+        wide = jnp.concatenate(parts, axis=1).astype(jnp.bfloat16)
+        h_ref[...] = dot(w1, wide).astype(jnp.bfloat16)
+
+    def reduce(base, h_ref):
+        h = h_ref[...]
+        u = dot(w2, h + h * jnp.tanh(h * (h * h + cg)))
+        for i in range(GROUP):
+            u_ref[pl.ds(base + i, channels, stride=t_step), :] = u[:, i * LANES : (i + 1) * LANES]
+
+    expand(0, h0_ref)
+
+    @pl.loop(0, rows // (2 * GROUP))
+    def _(g):
+        base = g * 2 * GROUP
+        expand(base + GROUP, h1_ref)
+        reduce(base, h0_ref)
+        expand(lax.rem(base + 2 * GROUP, rows), h0_ref)
+        reduce(base + GROUP, h1_ref)
+
+
+def add_update(st_ref, u_ref, c):
+    rows = st_ref.shape[1]
+    new = st_ref[c].astype(jnp.float32) + u_ref[pl.ds(c * (rows + PAD), rows), :]
+    new = new.astype(jnp.bfloat16)
+    st_ref[c] = new
+    return new
+
+
+def add_updates(st_ref, u_ref):
+    @pl.loop(0, st_ref.shape[0] // 4)
+    def _(g):
+        for i in range(4):
+            add_update(st_ref, u_ref, g * 4 + i)
+
+
+def scaled_weights(ew, rw):
+    w1 = (ew.astype(jnp.float32) * GELU_S).T.astype(jnp.bfloat16)
+    return w1, (rw.astype(jnp.float32) * (0.5 / GELU_S)).astype(jnp.bfloat16)
+
+
+def lanes(m):
+    return pl.ds(pl.multiple_of(m * LANES, LANES), LANES)
+
+
+def tail_kernel(kept, x_ref, mixed_ref, a_hbm, iy_ref, ew_ref, rw_ref, out_ref, *scratch):
+    st, mx, a_ref, t_ref, u_ref, h0_ref, h1_ref, m_ref = scratch[:8]
+    load_sem, mixed_sem, a_sem, store_sem = scratch[8:]
+    chunks, _, rows, _ = st.shape
+
+    def load(m):
+        return pltpu.make_async_copy(x_ref.at[:, :, lanes(m)], st.at[m], load_sem.at[m])
+
+    def store(m):
+        return pltpu.make_async_copy(st.at[m], out_ref.at[:, :, lanes(m)], store_sem.at[m])
+
+    def mixed(i):
+        return pltpu.make_async_copy(mixed_ref.at[i], mx.at[i], mixed_sem.at[i])
+
+    whole_a = pltpu.make_async_copy(a_hbm, a_ref, a_sem)
+    whole_a.start()
+    for i in range(chunks - kept):
+        mixed(i).start()
+        load(kept + i).start()
+    for m in range(kept):
+        load(m).start()
+    w1, w2 = scaled_weights(ew_ref[...], rw_ref[...])
+    whole_a.wait()
+
+    @pl.loop(kept, chunks)
+    def _(m):
+        mixed(m - kept).wait()
+        transform(mx.at[m - kept], a_ref, iy_ref[:, lanes(m)], m_ref, t_ref)
+        pointwise(w1, w2, rows, t_ref, u_ref, h0_ref, h1_ref)
+        load(m).wait()
+        add_updates(st.at[m], u_ref)
+        store(m).start()
+
+        @pl.when(m == kept)
+        def _():
+            for other in range(kept):
+                load(other).wait()
+                store(other).start()
+
+    @pl.loop(0, chunks)
+    def _(m):
+        store(m).wait()
+
+
+def mega(layers, gx, gy, plan, state_ref, fx_ref, fy_ref, ixt_ref, iy_ref, spx_ref, spy_ref,
+         ew_ref, rw_ref, out_ref, mixed_out, a_out, *scratch):
+    early, period, gap, kept = plan
     scratch = list(scratch)
     st, sx, mx, sy, my, t_ref, u_ref, h0_ref, h1_ref, m_ref, acc_ref, a_ref = scratch[:12]
     matx_ref, maty_ref, w1_ref, w2_ref = scratch[12:16]
     bits_x, bits_y = gx.bit_length() - 1, gy.bit_length() - 1
     rx = scratch[16 : 16 + bits_x]
     ry = scratch[16 + bits_x : 16 + bits_x + bits_y]
-    sendx, recvx, sendy, recvy, load_sem, store_sem = scratch[16 + bits_x + bits_y :]
+    sendx, recvx, sendy, recvy, load_sem, store_sem, mixed_sem, a_sem = scratch[16 + bits_x + bits_y :]
     chunks, channels, rows, _ = st.shape
     rows2 = fx_ref.shape[0]
     per_x, per_y = rows2 // gx, rows2 // gy
@@ -155,8 +267,7 @@
 
     def prepare():
         for layer in range(layers):
-            w1_ref[layer] = (ew_ref[layer].astype(f32) * GELU_S).T.astype(bf16)
-            w2_ref[layer] = (rw_ref[layer].astype(f32) * (0.5 / GELU_S)).T.astype(bf16)
+            w1_ref[layer], w2_ref[layer] = scaled_weights(ew_ref[layer], rw_ref[layer])
             for source, target in ((spx_ref, matx_ref), (spy_ref, maty_ref)):
 
                 @pl.loop(0, source.shape[1])
@@ -165,14 +276,17 @@
                     target[layer, j, :channels] = jnp.concatenate([real, -imag], axis=1)
                     target[layer, j, channels:] = jnp.concatenate([imag, real], axis=1)
 
-    def lanes(m):
-        return pl.ds(pl.multiple_of(m * LANES, LANES), LANES)
-
     def load(m):
         return pltpu.make_async_copy(state_ref.at[:, :, lanes(m)], st.at[m], load_sem.at[m])
 
     def store(m):
         return pltpu.make_async_copy(st.at[m], out_ref.at[:, :, lanes(m)], store_sem.at[m])
+
+    def keep_mixed(i):
+        return pltpu.make_async_copy(mx.at[kept + i], mixed_out.at[i], mixed_sem.at[i])
+
+    def keep_a():
+        return pltpu.make_async_copy(a_ref, a_out, a_sem)
 
     def spectra(base, news, fx, fy):
         count = len(news)
@@ -230,52 +344,10 @@
                 a_ref[g * 8 + i] = jnp.concatenate([top, low], axis=0).T.astype(bf16)
 
     def layer_start(m):
-        for p in range(gx):
-            for r in range(per_x):
-                at = pl.ds((p * per_x + r) * m_step, channels)
-                m_ref[at, :] = mx[m, p, r].astype(f32)
-        iy = iy_ref[:, lanes(m)]
-
-        @pl.loop(0, channels // WIDE)
-        def _(g):
-            for i in range(WIDE):
-                c = g * WIDE + i
-                part = m_ref[pl.ds(c, rows2, stride=m_step), :].astype(bf16)
-                t_ref[pl.ds(c * t_step, rows), :] = dot(
-                    a_ref[c], jnp.concatenate([part, iy], axis=0)
-                )
+        transform(mx.at[m], a_ref, iy_ref[:, lanes(m)], m_ref, t_ref)
 
     def layer_rest(layer, m):
-        w1, w2 = w1_ref[layer], w2_ref[layer]
-        cg = jnp.bfloat16(GELU_A / GELU_S)
-
-        def expand(base, h_ref):
-            parts = [t_ref[pl.ds(base + i, channels, stride=t_step), :] for i in range(GROUP)]
-            h_ref[...] = dot(w1, jnp.concatenate(parts, axis=1).astype(bf16)).astype(bf16)
-
-        def reduce(base, h_ref):
-            h = h_ref[...]
-            u = dot(w2, h + h * jnp.tanh(h * (h * h + cg)))
-            for i in range(GROUP):
-                u_ref[pl.ds(base + i, channels, stride=t_step), :] = u[
-                    :, i * LANES : (i + 1) * LANES
-                ]
-
-        expand(0, h0_ref)
-
-        @pl.loop(0, rows // (2 * GROUP))
-        def _(g):
-            base = g * 2 * GROUP
-            expand(base + GROUP, h1_ref)
-            reduce(base, h0_ref)
-            expand(lax.rem(base + 2 * GROUP, rows), h0_ref)
-            reduce(base + GROUP, h1_ref)
-
-        def updated(c):
-            new = st[m, c].astype(f32) + u_ref[pl.ds(c * t_step, rows), :]
-            new = new.astype(bf16)
-            st[m, c] = new
-            return new
+        pointwise(w1_ref[layer], w2_ref[layer], rows, t_ref, u_ref, h0_ref, h1_ref)
 
         @pl.when(layer < layers - 1)
         def _():
@@ -285,17 +357,17 @@
             @pl.loop(0, channels // WIDE)
             def _(g):
                 base = g * WIDE
-                spectra(base, [updated(base + i) for i in range(WIDE)], fx, fy)
+                spectra(base, [add_update(st.at[m], u_ref, base + i) for i in range(WIDE)], fx, fy)
 
             send_spectra(m)
 
+        @pl.when((layer == layers - 2) & (m >= kept))
+        def _():
+            store(m).start()
+
         @pl.when(layer == layers - 1)
         def _():
-            @pl.loop(0, channels // 4)
-            def _(g):
-                for i in range(4):
-                    updated(g * 4 + i)
-
+            add_updates(st.at[m], u_ref)
             store(m).start()
 
     barrier = pltpu.get_barrier_semaphore()
@@ -312,28 +384,38 @@
     pl.semaphore_wait(barrier, ex.bits + ey.bits)
 
     prepare()
-    early = pl.cdiv(chunks, 2)
-    period = max(chunks, ex.stages, early + 1 + ey.stages)
-
-    @pl.loop(0, layers * period + chunks)
+    later = period + gap
+
+    def place(t):
+        after = jnp.maximum(t - period, 0)
+        turn = jnp.where(t < period, 0, 1 + after // later)
+        return turn, jnp.where(t < period, t, lax.rem(after, later))
+
+    @pl.loop(0, period + (layers - 1) * later + kept)
     def _(t):
-        turn, m = t // period, lax.rem(t, period)
+        turn, m = place(t)
 
         def advance(stage):
-            q = t - 1 - stage
-            layer, chunk = q // period, lax.rem(q, period)
-
-            @pl.when((q >= 0) & (chunk < chunks) & (layer < layers))
+            layer, chunk = place(t - 1 - stage)
+
+            @pl.when((t >= 1 + stage) & (chunk < chunks) & (layer < layers))
             def _():
                 ex.finish(stage, layer, chunk)
+                if stage == ex.stages - 1:
+
+                    @pl.when((layer == layers - 1) & (chunk >= kept))
+                    def _():
+                        keep_mixed(chunk - kept).start()
 
         if ex.stages:
             advance(ex.stages - 1)
         for stage in range(ey.stages):
-
-            @pl.when((t == early + 1 + stage) | ((turn > 1) & (m == 0)))
+            left = ey.stages - 1 - stage
+            since = t - period + left
+
+            @pl.when((t == period - 2 * left) | ((since >= later) & (lax.rem(since, later) == 0)))
             def _():
-                ey.finish(stage, jnp.maximum(turn - 1, 0), 0)
+                ey.finish(stage, jnp.maximum(since, 0) // later, 0)
 
         for i in range(2):
 
@@ -345,6 +427,10 @@
         def _():
             build_a()
 
+            @pl.when(turn == layers)
+            def _():
+                keep_a().start()
+
         @pl.when((turn > 0) & (m < chunks))
         def _():
             layer_start(m)
@@ -359,6 +445,12 @@
     @pl.loop(0, chunks)
     def _(m):
         store(m).wait()
+
+    @pl.loop(0, chunks - kept)
+    def _(i):
+        keep_mixed(i).wait()
+
+    keep_a().wait()
 
 
 def body(state_field, spectral_x, spectral_y, expand_weight, reduce_weight):
@@ -388,10 +480,14 @@
         spectral_x,
         spectral_y,
         expand_weight,
-        reduce_weight,
+        jnp.swapaxes(reduce_weight, 1, 2),
     ]
     bits_x, bits_y = gx.bit_length() - 1, gy.bit_length() - 1
     per_x, per_y = rows2 // gx, rows2 // gy
+    early, gap = pl.cdiv(chunks, 2), 2
+    period = max(chunks, 2 * bits_x, early + 4 * bits_y - 1)
+    kept = max(0, chunks - 2, chunks + 2 * bits_x - period - gap)
+    tail = chunks - kept
     m_rows = max(channels, rows2) * (max(channels, rows2) + PAD)
     scratch = [
         pltpu.VMEM((chunks, channels, rows, LANES), bf16),
@@ -417,19 +513,45 @@
         scratch.append(pltpu.VMEM((1, gy >> (s + 1), per_y, channels, rows), bf16))
     dma = pltpu.SemaphoreType.DMA
     scratch += [dma((2 * bits_x, chunks))] * 2 + [dma((2 * bits_y, 1))] * 2 + [dma((chunks,))] * 2
+    scratch += [dma((chunks - kept,)), dma(())]
     vmem = pl.BlockSpec(memory_space=pltpu.VMEM)
     anywhere = pl.BlockSpec(memory_space=pl.ANY)
-    out = pl.pallas_call(
-        functools.partial(mega, layers, gx, gy),
+    state_shape = jax.ShapeDtypeStruct((channels, rows, cols), bf16)
+    mixed_shape = jax.ShapeDtypeStruct((tail, gx, per_x, channels, LANES), bf16)
+    a_shape = jax.ShapeDtypeStruct((channels, rows, 2 * rows2), bf16)
+    state, mixed, a = pl.pallas_call(
+        functools.partial(mega, layers, gx, gy, (early, period, gap, kept)),
         name="layers",
-        out_shape=jax.ShapeDtypeStruct((channels, rows, cols), bf16),
+        out_shape=[state_shape, mixed_shape, a_shape],
         in_specs=[anywhere] + [vmem] * (len(args) - 1),
-        out_specs=anywhere,
+        out_specs=[anywhere] * 3,
         scratch_shapes=scratch,
         compiler_params=pltpu.CompilerParams(
             collective_id=0, has_side_effects=True, vmem_limit_bytes=67043328
         ),
     )(*args)
+    out = pl.pallas_call(
+        functools.partial(tail_kernel, kept),
+        name="tail",
+        out_shape=state_shape,
+        in_specs=[anywhere] * 3 + [vmem] * 3,
+        out_specs=anywhere,
+        scratch_shapes=[
+            pltpu.VMEM((chunks, channels, rows, LANES), bf16),
+            pltpu.VMEM(mixed_shape.shape, bf16),
+            pltpu.VMEM(a_shape.shape, bf16),
+            pltpu.VMEM((channels * (rows + PAD), LANES), f32),
+            pltpu.VMEM((channels * (rows + PAD), LANES), f32),
+            pltpu.VMEM((hidden, GROUP * LANES), bf16),
+            pltpu.VMEM((hidden, GROUP * LANES), bf16),
+            pltpu.VMEM((m_rows, LANES), f32),
+            dma((chunks,)),
+            dma((tail,)),
+            dma(()),
+            dma((chunks,)),
+        ],
+        compiler_params=pltpu.CompilerParams(vmem_limit_bytes=60 * 1024 * 1024),
+    )(state, mixed, a, inverse_y, expand_weight[-1], args[-1][-1])
     return out.reshape(state_field.shape)
 
 

time: 275 us -> 258 us (0.938)
  local copies, waits for them, and re-layouts: 15.5 us -> 1.4 us
  Pallas kernels: 255 us -> 252 us
    unnamed x2 -> x0, local copies, waits for them, and re-layouts: 15.5 us -> none
    pallas_call x1 -> x2, Pallas kernels: 255 us -> 252 us  [the longest x1 230 us: body(): pl.pallas_call(functools.partial(mega, layers, gx, gy, (early, period, ga...]
where the time goes in v5:
time: 258 us; the launch traced here: 257 us
  Pallas kernels  252 us (98%)
  other arithmetic  4.1 us (2%)
    pallas_call x1, Pallas kernels, body(): pl.pallas_call(functools.partial(mega, layers, gx, gy, (early, period, ga...  230 us
    pallas_call x1, Pallas kernels, body(): pl.pallas_call(functools.partial(tail_kernel, kept), name='tail', out_sha...  22.4 us

profile of v5, /device:TPU:0, one launch (start us, length us, event | category | flops | bytes accessed | tf_op | source)
XLA Modules:
  0.0 257.4 jit_solution(3202367180728187059)
XLA Ops:
  0.0 1.5 multiply_convert_fusion.2
  1.5 1.4 slice_bitcast_fusion
  2.9 2.6 %multiply_convert_fusion = (bf16[64,1024]{1,0:T(8,128)(2,1)}, bf16[64,1024]{1,0:T(8,128)(2,1)}) fusion(f32[64]{0:T(128)} %constant.78, s32[1024]{0:T(1024)S(1)} %iota_add_fusion, s32[64]{0:T(128)} %constant.74.clone, s32[64]{0:T(128)S(1)} %get-tuple-element.15, s32[64]{0:T(128)S(1)} %get-tuple-element.16, pred[64]{0:T(512)(128)(4,1)S(1)} %compare_and_fusion), kind=kLoop, calls=%fused_computation.8 | loop fusion | flops 1441792 | bytes 267328 | tf_op jit(solution)/shard_map/convert_element_type | solution.py:39
  5.5 229.6 %layers.1 = (bf16[64,128,1024]{2,1,0:T(8,128)(2,1)}, bf16[2,16,4,64,128]{4,3,2,1,0:T(8,128)(2,1)}, bf16[64,128,128]{2,1,0:T(8,128)(2,1)}) custom-call(bf16[64,128,1024]{2,1,0:T(8,128)(2,1)} %bitcast.7, bf16[64,128]{1,0:T(8,128)(2,1)} %get-tuple-element.14.fx_ref, bf16[64,1024]{1,0:T(8,128)(2,1)} %get-tuple-element.12.fy_ref, ...), custom_call_target="tpu_custom_call" | custom-call | tf_op jit(solution)/shard_map/layers/pallas_call | solution.py:522
  235.1 22.4 %tail.1 = bf16[64,128,1024]{2,1,0:T(8,128)(2,1)} custom-call(bf16[64,128,1024]{2,1,0:T(8,128)(2,1)} %get-tuple-element.8.x_ref, bf16[2,16,4,64,128]{4,3,2,1,0:T(8,128)(2,1)} %get-tuple-element.9.mixed_ref, bf16[64,128,128]{2,1,0:T(8,128)(2,1)} %get-tuple-element.10.a_hbm, bf16[64,1024]{1,0:T(8,128)(2,1)} %get-tuple-element.11.iy_ref, ...), custom_call_target="tpu_custom_call" | custom-call | tf_op jit(solution)/shard_map/tail/pallas_call | solution.py:533
  (4 shorter events, 0.0 us)

commit v6 on v5

--- a/solution.py
+++ b/solution.py
@@ -10,6 +10,7 @@
 LANES = 128
 PAD = 4
 GROUP = 8
+FIRST = 3
 WIDE = 16
 GELU_A = 0.7978845608028654
 GELU_B = 0.044715
@@ -32,9 +33,9 @@
     positions = first + jnp.arange(count, dtype=jnp.int32)
     orders = jnp.array([k for k in order for _ in range(2)], dtype=jnp.int32)[:, None]
     part = lax.broadcasted_iota(jnp.int32, (rows2, count), 0) % 2
-    angle = 2.0 * jnp.pi * (orders * positions[None, :] % length).astype(jnp.float32) / length
+    steps = (4 * orders * positions[None, :] + part * length) % (4 * length)
     factor = 1.0 / jnp.sqrt(jnp.float32(length))
-    forward = jnp.where(part == 0, jnp.cos(angle), -jnp.sin(angle)) * factor
+    forward = jnp.cos(jnp.pi * steps.astype(jnp.float32) / (2 * length)) * factor
     inverse = jnp.where(orders == 0, 1.0, 2.0) * forward
     return forward.astype(jnp.bfloat16), inverse.astype(jnp.bfloat16)
 
@@ -49,11 +50,27 @@
     )
 
 
+def stage_ends(stages):
+    spans = [2 if stages >= 4 and s in (1, stages - 2) else 1 for s in range(stages)]
+    return [sum(spans[: s + 1]) for s in range(stages)]
+
+
 def stage_order(stages):
-    first = [0, stages - 3] if stages >= 4 else []
-    late = [1, stages - 2] if stages >= 4 else []
-    middle = [s for s in reversed(range(stages - 1)) if s not in first + late]
-    return list(dict.fromkeys(first + middle + late)) + [stages - 1]
+    if stages < 4:
+        return list(reversed(range(stages)))
+    first, late = [stages - 1, stages - 3, 0], [stages - 2, 1]
+    middle = [s for s in reversed(range(stages)) if s not in first + late]
+    return list(dict.fromkeys(first + middle + late))
+
+
+def schedule(chunks, stages, y_stages):
+    late = (stage_ends(stages)[-1] + 1) // 2 if stages else 0
+    early = pl.cdiv(chunks, FIRST)
+    first = max(late, early + max(y_stages - 1, 0), 1)
+    base = max(chunks, first + 1)
+    second = max(first + chunks + y_stages, base + late)
+    kept = min(chunks, max(0, chunks - 2, base + chunks + late - second))
+    return first, second - first, base, kept
 
 
 class Exchange:
@@ -139,7 +156,9 @@
             t_ref[pl.ds(c * t_step, rows), :] = dot(a_ref[c], jnp.concatenate([part, iy], axis=0))
 
 
-def pointwise(w1, w2, rows, t_ref, u_ref, h0_ref, h1_ref):
+def pointwise(w1, w2, rows, t_ref, u_ref, h0_ref, h1_ref, begin=True, end=True):
+    steps = rows // (2 * GROUP)
+    low, high = (0 if begin else steps // 2), (steps if end else steps // 2)
     channels, t_step = w2.shape[0], rows + PAD
     cg = jnp.bfloat16(GELU_A / GELU_S)
 
@@ -154,9 +173,10 @@
         for i in range(GROUP):
             u_ref[pl.ds(base + i, channels, stride=t_step), :] = u[:, i * LANES : (i + 1) * LANES]
 
-    expand(0, h0_ref)
-
-    @pl.loop(0, rows // (2 * GROUP))
+    if begin:
+        expand(0, h0_ref)
+
+    @pl.loop(low, high)
     def _(g):
         base = g * 2 * GROUP
         expand(base + GROUP, h1_ref)
@@ -210,7 +230,7 @@
         load(kept + i).start()
     for m in range(kept):
         load(m).start()
-    w1, w2 = scaled_weights(ew_ref[...], rw_ref[...])
+    w1, w2 = scaled_weights(ew_ref[ew_ref.shape[0] - 1], rw_ref[rw_ref.shape[0] - 1])
     whole_a.wait()
 
     @pl.loop(kept, chunks)
@@ -235,7 +255,7 @@
 
 def mega(layers, gx, gy, plan, state_ref, fx_ref, fy_ref, ixt_ref, iy_ref, spx_ref, spy_ref,
          ew_ref, rw_ref, out_ref, mixed_out, a_out, *scratch):
-    early, period, gap, kept = plan
+    first, later, base, kept = plan
     scratch = list(scratch)
     st, sx, mx, sy, my, t_ref, u_ref, h0_ref, h1_ref, m_ref, acc_ref, a_ref = scratch[:12]
     matx_ref, maty_ref, w1_ref, w2_ref = scratch[12:16]
@@ -343,11 +363,15 @@
                 low = acc_ref[pl.ds(g * 8 + i, rows2, stride=m_step), :]
                 a_ref[g * 8 + i] = jnp.concatenate([top, low], axis=0).T.astype(bf16)
 
-    def layer_start(m):
+    def layer_start(layer, m):
         transform(mx.at[m], a_ref, iy_ref[:, lanes(m)], m_ref, t_ref)
+        network(layer, end=False)
+
+    def network(layer, **part):
+        pointwise(w1_ref[layer], w2_ref[layer], rows, t_ref, u_ref, h0_ref, h1_ref, **part)
 
     def layer_rest(layer, m):
-        pointwise(w1_ref[layer], w2_ref[layer], rows, t_ref, u_ref, h0_ref, h1_ref)
+        network(layer, begin=False)
 
         @pl.when(layer < layers - 1)
         def _():
@@ -384,44 +408,45 @@
     pl.semaphore_wait(barrier, ex.bits + ey.bits)
 
     prepare()
-    later = period + gap
-
-    def place(t):
-        after = jnp.maximum(t - period, 0)
-        turn = jnp.where(t < period, 0, 1 + after // later)
-        return turn, jnp.where(t < period, t, lax.rem(after, later))
-
-    @pl.loop(0, period + (layers - 1) * later + kept)
+    ends = stage_ends(ex.stages)
+
+    def place(t, start):
+        after = jnp.maximum(t - start, 0)
+        turn = jnp.where(t < start, 0, 1 + after // later)
+        return turn, jnp.where(t < start, t, lax.rem(after, later))
+
+    @pl.loop(0, first + (layers - 1) * later + kept)
     def _(t):
-        turn, m = place(t)
-
-        def advance(stage):
-            layer, chunk = place(t - 1 - stage)
-
-            @pl.when((t >= 1 + stage) & (chunk < chunks) & (layer < layers))
-            def _():
-                ex.finish(stage, layer, chunk)
-                if stage == ex.stages - 1:
-
-                    @pl.when((layer == layers - 1) & (chunk >= kept))
+        turn, m = place(t, first)
+
+        def advance(half):
+            for stage in stage_order(ex.stages):
+                if ends[stage] % 2 == half:
+                    ago = ends[stage] // 2
+                    layer, chunk = place(t - ago, base)
+
+                    @pl.when((t >= ago) & (chunk < chunks) & (layer < layers))
                     def _():
-                        keep_mixed(chunk - kept).start()
-
-        if ex.stages:
-            advance(ex.stages - 1)
+                        ex.finish(stage, layer, chunk)
+                        if stage == ex.stages - 1:
+
+                            @pl.when((layer == layers - 1) & (chunk >= kept))
+                            def _():
+                                keep_mixed(chunk - kept).start()
+
+        advance(0)
         for stage in range(ey.stages):
-            left = ey.stages - 1 - stage
-            since = t - period + left
-
-            @pl.when((t == period - 2 * left) | ((since >= later) & (lax.rem(since, later) == 0)))
+            since = t - first + ey.stages - 1 - stage
+
+            @pl.when((since >= 0) & (lax.rem(jnp.maximum(since, 0), later) == 0))
             def _():
                 ey.finish(stage, jnp.maximum(since, 0) // later, 0)
 
-        for i in range(2):
-
-            @pl.when(2 * t + i < chunks)
+        for i in range(FIRST):
+
+            @pl.when(FIRST * t + i < chunks)
             def _():
-                first_task(2 * t + i)
+                first_task(FIRST * t + i)
 
         @pl.when((turn > 0) & (m == 0))
         def _():
@@ -433,10 +458,9 @@
 
         @pl.when((turn > 0) & (m < chunks))
         def _():
-            layer_start(m)
-
-        for stage in stage_order(ex.stages)[:-1] if ex.stages else []:
-            advance(stage)
+            layer_start(turn - 1, m)
+
+        advance(1)
 
         @pl.when((turn > 0) & (m < chunks))
         def _():
@@ -484,9 +508,8 @@
     ]
     bits_x, bits_y = gx.bit_length() - 1, gy.bit_length() - 1
     per_x, per_y = rows2 // gx, rows2 // gy
-    early, gap = pl.cdiv(chunks, 2), 2
-    period = max(chunks, 2 * bits_x, early + 4 * bits_y - 1)
-    kept = max(0, chunks - 2, chunks + 2 * bits_x - period - gap)
+    plan = schedule(chunks, 2 * bits_x, 2 * bits_y)
+    kept = plan[-1]
     tail = chunks - kept
     m_rows = max(channels, rows2) * (max(channels, rows2) + PAD)
     scratch = [
@@ -520,7 +543,7 @@
     mixed_shape = jax.ShapeDtypeStruct((tail, gx, per_x, channels, LANES), bf16)
     a_shape = jax.ShapeDtypeStruct((channels, rows, 2 * rows2), bf16)
     state, mixed, a = pl.pallas_call(
-        functools.partial(mega, layers, gx, gy, (early, period, gap, kept)),
+        functools.partial(mega, layers, gx, gy, plan),
         name="layers",
         out_shape=[state_shape, mixed_shape, a_shape],
         in_specs=[anywhere] + [vmem] * (len(args) - 1),
@@ -551,7 +574,7 @@
             dma((chunks,)),
         ],
         compiler_params=pltpu.CompilerParams(vmem_limit_bytes=60 * 1024 * 1024),
-    )(state, mixed, a, inverse_y, expand_weight[-1], args[-1][-1])
+    )(state, mixed, a, inverse_y, *args[-2:])
     return out.reshape(state_field.shape)
 
 

time: 258 us -> 254 us (0.984)
  no operation moved by 1% of the time
where the time goes in v6:
time: 254 us
  Pallas kernels  250 us (98%)
  other arithmetic  4.01 us (2%)
    pallas_call x1, Pallas kernels, body(): pl.pallas_call(functools.partial(mega, layers, gx, gy, plan), name='layer...  228 us
    pallas_call x1, Pallas kernels, body(): pl.pallas_call(functools.partial(tail_kernel, kept), name='tail', out_sha...  22.4 us

profile of v6, /device:TPU:0, one launch (start us, length us, event | category | flops | bytes accessed | tf_op | source)
XLA Modules:
  0.0 254.0 jit_solution(13089094721112612185)
XLA Ops:
  0.0 1.5 multiply_convert_fusion.2
  1.5 2.5 multiply_convert_fusion
  4.0 227.6 %layers.1 = (bf16[64,128,1024]{2,1,0:T(8,128)(2,1)}, bf16[2,16,4,64,128]{4,3,2,1,0:T(8,128)(2,1)}, bf16[64,128,128]{2,1,0:T(8,128)(2,1)}) custom-call(bf16[64,128,1024]{2,1,0:T(8,128)(2,1)} %bitcast.3, bf16[64,128]{1,0:T(8,128)(2,1)} %get-tuple-element.14.fx_ref, bf16[64,1024]{1,0:T(8,128)(2,1)} %get-tuple-element.12.fy_ref, ...), custom_call_target="tpu_custom_call" | custom-call | tf_op jit(solution)/shard_map/layers/pallas_call | solution.py:545
  231.6 22.4 %tail.1 = bf16[64,128,1024]{2,1,0:T(8,128)(2,1)} custom-call(bf16[64,128,1024]{2,1,0:T(8,128)(2,1)} %get-tuple-element.8.x_ref, bf16[2,16,4,64,128]{4,3,2,1,0:T(8,128)(2,1)} %get-tuple-element.9.mixed_ref, bf16[64,128,128]{2,1,0:T(8,128)(2,1)} %get-tuple-element.10.a_hbm, bf16[64,1024]{1,0:T(8,128)(2,1)} %get-tuple-element.11.iy_ref, ...), custom_call_target="tpu_custom_call" | custom-call | tf_op jit(solution)/shard_map/tail/pallas_call | solution.py:556
  (4 shorter events, 0.0 us)

commit v7 on v6

--- a/solution.py
+++ b/solution.py
@@ -51,7 +51,7 @@
 
 
 def stage_ends(stages):
-    spans = [2 if stages >= 4 and s in (1, stages - 2) else 1 for s in range(stages)]
+    spans = [2 if stages >= 4 and s in (1, stages // 2 - 1, stages // 2, stages - 2) else 1 for s in range(stages)]
     return [sum(spans[: s + 1]) for s in range(stages)]
 
 
@@ -68,7 +68,7 @@
     early = pl.cdiv(chunks, FIRST)
     first = max(late, early + max(y_stages - 1, 0), 1)
     base = max(chunks, first + 1)
-    second = max(first + chunks + y_stages, base + late)
+    second = max(first + chunks + y_stages, base + late + 1)
     kept = min(chunks, max(0, chunks - 2, base + chunks + late - second))
     return first, second - first, base, kept
 
@@ -407,7 +407,6 @@
 
     pl.semaphore_wait(barrier, ex.bits + ey.bits)
 
-    prepare()
     ends = stage_ends(ex.stages)
 
     def place(t, start):
@@ -461,6 +460,10 @@
             layer_start(turn - 1, m)
 
         advance(1)
+
+        @pl.when(t == 0)
+        def _():
+            prepare()
 
         @pl.when((turn > 0) & (m < chunks))
         def _():

time: 254 us -> 251 us (0.988)
  Pallas kernels: 250 us -> 247 us
    pallas_call x1, Pallas kernels: 228 us -> 224 us  [body(): pl.pallas_call(functools.partial(mega, layers, gx, gy, plan), name='layer...]
where the time goes in v7:
time: 251 us
  Pallas kernels  247 us (98%)
  other arithmetic  4.01 us (2%)
    pallas_call x1, Pallas kernels, body(): pl.pallas_call(functools.partial(mega, layers, gx, gy, plan), name='layer...  224 us
    pallas_call x1, Pallas kernels, body(): pl.pallas_call(functools.partial(tail_kernel, kept), name='tail', out_sha...  22.4 us

profile of v7, /device:TPU:0, one launch (start us, length us, event | category | flops | bytes accessed | tf_op | source)
XLA Modules:
  0.0 250.6 jit_solution(4026058072671453902)
XLA Ops:
  0.0 1.5 multiply_convert_fusion.2
  1.5 2.5 multiply_convert_fusion
  4.0 224.2 %layers.1 = (bf16[64,128,1024]{2,1,0:T(8,128)(2,1)}, bf16[2,16,4,64,128]{4,3,2,1,0:T(8,128)(2,1)}, bf16[64,128,128]{2,1,0:T(8,128)(2,1)}) custom-call(bf16[64,128,1024]{2,1,0:T(8,128)(2,1)} %bitcast.3, bf16[64,128]{1,0:T(8,128)(2,1)} %get-tuple-element.14.fx_ref, bf16[64,1024]{1,0:T(8,128)(2,1)} %get-tuple-element.12.fy_ref, ...), custom_call_target="tpu_custom_call" | custom-call | tf_op jit(solution)/shard_map/layers/pallas_call | solution.py:548
  228.2 22.4 %tail.1 = bf16[64,128,1024]{2,1,0:T(8,128)(2,1)} custom-call(bf16[64,128,1024]{2,1,0:T(8,128)(2,1)} %get-tuple-element.8.x_ref, bf16[2,16,4,64,128]{4,3,2,1,0:T(8,128)(2,1)} %get-tuple-element.9.mixed_ref, bf16[64,128,128]{2,1,0:T(8,128)(2,1)} %get-tuple-element.10.a_hbm, bf16[64,1024]{1,0:T(8,128)(2,1)} %get-tuple-element.11.iy_ref, ...), custom_call_target="tpu_custom_call" | custom-call | tf_op jit(solution)/shard_map/tail/pallas_call | solution.py:559
  (4 shorter events, 0.0 us)

commit v8 on v7

--- a/solution.py
+++ b/solution.py
@@ -10,7 +10,7 @@
 LANES = 128
 PAD = 4
 GROUP = 8
-FIRST = 3
+FIRST = 2
 WIDE = 16
 GELU_A = 0.7978845608028654
 GELU_B = 0.044715

time: 251 us -> 249 us (level)
  no operation moved by 1% of the time
where the time goes in v8:
time: 249 us
  Pallas kernels  245 us (98%)
  other arithmetic  4.01 us (2%)
    pallas_call x1, Pallas kernels, body(): pl.pallas_call(functools.partial(mega, layers, gx, gy, plan), name='layer...  223 us
    pallas_call x1, Pallas kernels, body(): pl.pallas_call(functools.partial(tail_kernel, kept), name='tail', out_sha...  22.4 us

profile of v8, /device:TPU:0, one launch (start us, length us, event | category | flops | bytes accessed | tf_op | source)
XLA Modules:
  0.0 249.1 jit_solution(14471630575182103486)
XLA Ops:
  0.0 1.5 multiply_convert_fusion.2
  1.5 2.5 multiply_convert_fusion
  4.0 222.7 %layers.1 = (bf16[64,128,1024]{2,1,0:T(8,128)(2,1)}, bf16[2,16,4,64,128]{4,3,2,1,0:T(8,128)(2,1)}, bf16[64,128,128]{2,1,0:T(8,128)(2,1)}) custom-call(bf16[64,128,1024]{2,1,0:T(8,128)(2,1)} %bitcast.3, bf16[64,128]{1,0:T(8,128)(2,1)} %get-tuple-element.14.fx_ref, bf16[64,1024]{1,0:T(8,128)(2,1)} %get-tuple-element.12.fy_ref, ...), custom_call_target="tpu_custom_call" | custom-call | tf_op jit(solution)/shard_map/layers/pallas_call | solution.py:548
  226.8 22.4 %tail.1 = bf16[64,128,1024]{2,1,0:T(8,128)(2,1)} custom-call(bf16[64,128,1024]{2,1,0:T(8,128)(2,1)} %get-tuple-element.8.x_ref, bf16[2,16,4,64,128]{4,3,2,1,0:T(8,128)(2,1)} %get-tuple-element.9.mixed_ref, bf16[64,128,128]{2,1,0:T(8,128)(2,1)} %get-tuple-element.10.a_hbm, bf16[64,1024]{1,0:T(8,128)(2,1)} %get-tuple-element.11.iy_ref, ...), custom_call_target="tpu_custom_call" | custom-call | tf_op jit(solution)/shard_map/tail/pallas_call | solution.py:559
  (4 shorter events, 0.0 us)

commit v9 on v8

--- a/solution.py
+++ b/solution.py
@@ -68,7 +68,7 @@
     early = pl.cdiv(chunks, FIRST)
     first = max(late, early + max(y_stages - 1, 0), 1)
     base = max(chunks, first + 1)
-    second = max(first + chunks + y_stages, base + late + 1)
+    second = max(first + chunks + max(y_stages - 1, 0), base + late + 1)
     kept = min(chunks, max(0, chunks - 2, base + chunks + late - second))
     return first, second - first, base, kept
 

time: 249 us -> 253 us (1.016)
  Pallas kernels: 245 us -> 249 us
    pallas_call x1, Pallas kernels: 223 us -> 229 us  [body(): pl.pallas_call(functools.partial(mega, layers, gx, gy, plan), name='layer...]
where the time goes in v9:
time: 253 us
  Pallas kernels  249 us (98%)
  other arithmetic  4.01 us (2%)
    pallas_call x1, Pallas kernels, body(): pl.pallas_call(functools.partial(mega, layers, gx, gy, plan), name='layer...  229 us
    pallas_call x1, Pallas kernels, body(): pl.pallas_call(functools.partial(tail_kernel, kept), name='tail', out_sha...  20 us

profile of v9, /device:TPU:0, one launch (start us, length us, event | category | flops | bytes accessed | tf_op | source)
XLA Modules:
  0.0 252.8 jit_solution(7091695659661025045)
XLA Ops:
  0.0 1.5 multiply_convert_fusion.2
  1.5 2.5 multiply_convert_fusion
  4.0 228.8 %layers.1 = (bf16[64,128,1024]{2,1,0:T(8,128)(2,1)}, bf16[1,16,4,64,128]{4,3,2,1,0:T(8,128)(2,1)}, bf16[64,128,128]{2,1,0:T(8,128)(2,1)}) custom-call(bf16[64,128,1024]{2,1,0:T(8,128)(2,1)} %bitcast.3, bf16[64,128]{1,0:T(8,128)(2,1)} %get-tuple-element.14.fx_ref, bf16[64,1024]{1,0:T(8,128)(2,1)} %get-tuple-element.12.fy_ref, ...), custom_call_target="tpu_custom_call" | custom-call | tf_op jit(solution)/shard_map/layers/pallas_call | solution.py:548
  232.8 20.0 %tail.1 = bf16[64,128,1024]{2,1,0:T(8,128)(2,1)} custom-call(bf16[64,128,1024]{2,1,0:T(8,128)(2,1)} %get-tuple-element.8.x_ref, bf16[1,16,4,64,128]{4,3,2,1,0:T(8,128)(2,1)} %get-tuple-element.9.mixed_ref, bf16[64,128,128]{2,1,0:T(8,128)(2,1)} %get-tuple-element.10.a_hbm, bf16[64,1024]{1,0:T(8,128)(2,1)} %get-tuple-element.11.iy_ref, ...), custom_call_target="tpu_custom_call" | custom-call | tf_op jit(solution)/shard_map/tail/pallas_call | solution.py:559
  (4 shorter events, 0.0 us)
